TPU v7x, 512 devices: a whole 4x4x16 slice. The times are simulated.
512 devices in a mesh: fsdp: 8 (over y_lo, x), ctx: 64 (over y_hi, z, core).
Axes of the slice: x: 4, y: 4 (y_hi: 2, y_lo: 2; y = y_hi * 2 + y_lo), z: 16, core: 2. Of those that a mesh axis runs over, the one named last changes fastest.
Arguments:
- latents: float32 [8192, 64], P('ctx'), may hold values from -15 to 15
- stream: bfloat16 [8192, 3072], P('ctx'), may hold values from -6 to 6
- queries: bfloat16 [8192, 2048], P('ctx', 'fsdp'), may hold values from -200 to 200
- key_rows: bfloat16 [8192, 2048], P('ctx', 'fsdp'), may hold values from -4 to 4
- value_rows: bfloat16 [8192, 2048], P('ctx', 'fsdp'), may hold values from -6 to 6
- w_mix: bfloat16 [2048, 3072], P('fsdp', 'ctx'), may hold values from -0.25 to 0.25
- w_head: bfloat16 [3072, 128], P('fsdp'), may hold values from -0.0390625 to 0.0390625
Outputs:
- flipped: float32 [8192, 64], P('ctx')
- head_grad: float32 [3072, 128], P('fsdp')
All inputs are finite; a program needn't handle non-finite values.
Results may differ from a plain program's by a relative error of at most 0.003.
The roundings to bfloat16 on the way count: a program that leaves them out, or rounds other values in their place, can miss the bound.
Values may be sent and summed in bfloat16 or wider, within the bound.
A program may use at most 64 MiB of HBM per device.

v0:
```python
import jax
import jax.numpy as jnp
from jax import lax
from jax.sharding import PartitionSpec as P

HD = 128


def shifted(shard, axis, by):
    devices = lax.axis_size(axis)
    pairs = [(i, i + by) for i in range(devices) if 0 <= i + by < devices]
    return lax.ppermute(shard, axis, pairs)


def fold_block(partial_value, block_kv, offset, query_heads, query_pos):
    key_part, value_part = block_kv
    piece_len = key_part.shape[0]
    heads_here = query_heads.shape[1]

    def compute(current):
        old_max, old_sum, old_acc = current
        key_heads = key_part.reshape(piece_len, heads_here, HD)
        value_heads = value_part.reshape(piece_len, heads_here, HD)
        scores = jnp.einsum(
            "qhd,khd->hqk", query_heads, key_heads, preferred_element_type=jnp.float32
        ) * HD ** (-0.5)
        key_pos = jnp.arange(piece_len, dtype=jnp.int32)
        causal = key_pos[None, :] <= query_pos[:, None]
        scores = jnp.where(causal[None], scores, -1e30)
        new_max = jnp.maximum(old_max, jnp.max(scores, axis=-1))
        weights = jnp.where(causal[None], jnp.exp(scores - new_max[..., None]), 0.0)
        new_sum = jnp.sum(weights, axis=-1)
        update = jnp.einsum(
            "hqk,khd->hqd",
            weights.astype(jnp.bfloat16),
            value_heads,
            preferred_element_type=jnp.float32,
        )
        return (new_max, new_sum, update)

    def passed(current):
        return current

    return lax.cond(offset <= jnp.max(query_pos), compute, passed, partial_value)


def empty_state(heads_here, num_rows):
    return (
        jnp.full((heads_here, num_rows), -1e30, jnp.float32),
        jnp.zeros((heads_here, num_rows), jnp.float32),
        jnp.zeros((heads_here, num_rows, HD), jnp.float32),
    )


def finish(current):
    output = current[2] / current[1][..., None]
    heads_here, num_rows = current[1].shape
    return jnp.transpose(output, (1, 0, 2)).reshape(num_rows, heads_here * HD).astype(jnp.bfloat16)


def shards(latents, stream, queries, key_rows, value_rows, w_mix, w_head):
    tok_rows = queries.shape[0]
    heads_here = queries.shape[1] // HD
    channels = latents.shape[1]
    ctx_count = lax.axis_size("ctx")
    ctx_index = lax.axis_index("ctx")
    row_base = ctx_index * tok_rows
    own_heads = queries.reshape(tok_rows, heads_here, HD)
    own_pos = row_base + jnp.arange(tok_rows, dtype=jnp.int32)
    result_state = fold_block(
        empty_state(heads_here, tok_rows),
        (
            lax.all_gather(key_rows, "ctx", axis=0, tiled=True),
            lax.all_gather(value_rows, "ctx", axis=0, tiled=True),
        ),
        jnp.int32(0),
        own_heads,
        own_pos,
    )
    attended = finish(result_state)
    fsdp_count = lax.axis_size("fsdp")
    fsdp_index = lax.axis_index("fsdp")
    model_width = stream.shape[1]
    share_cols = model_width // fsdp_count
    mixed_part = jnp.dot(
        attended,
        lax.all_gather(w_mix, "ctx", axis=1, tiled=True),
        preferred_element_type=jnp.float32,
    )
    mixed = lax.psum(mixed_part, "fsdp")
    resid = stream.astype(jnp.float32) + mixed
    head_full = lax.all_gather(w_head, "fsdp", axis=0, tiled=True)
    pred = jnp.dot(resid, head_full.astype(jnp.float32), precision=lax.Precision.HIGHEST)
    resid_mine = lax.dynamic_slice_in_dim(resid, fsdp_index * share_cols, share_cols, 1)
    before = shifted(pred[tok_rows - 1 :], "ctx", 1)
    prior = jnp.concatenate([before, pred[:-1]], axis=0)
    shift_part = prior[:, :channels]
    log_scale = prior[:, channels:]
    inverse = jnp.exp(-log_scale)
    white = (latents - shift_part) * inverse
    loss_scale = float(tok_rows * ctx_count) ** (-0.5)
    d_prior = jnp.concatenate([-white * inverse, 1.0 - white * white], axis=1) * loss_scale
    after = shifted(d_prior[:1], "ctx", -1)
    d_pred = jnp.concatenate([d_prior[1:], after], axis=0)
    grad_part = jnp.dot(resid_mine.T, d_pred, precision=lax.Precision.HIGHEST)
    head_grad = lax.psum(grad_part, "ctx")
    piece_rows = tok_rows // ctx_count

    def mirror_step(pieces):
        return lax.all_to_all(pieces, "ctx", split_axis=0, concat_axis=0, tiled=True)

    first_pass = mirror_step(white.reshape(ctx_count, piece_rows, channels))
    second_pass = mirror_step(first_pass[::-1, ::-1])
    flipped = second_pass[::-1].reshape(tok_rows, channels)
    return (flipped, head_grad)


def solution(mesh):
    return jax.shard_map(
        shards,
        mesh=mesh,
        in_specs=(
            P("ctx", None),
            P("ctx", None),
            P("ctx", "fsdp"),
            P("ctx", "fsdp"),
            P("ctx", "fsdp"),
            P("fsdp", "ctx"),
            P("fsdp", None),
        ),
        out_specs=(P("ctx", None), P("fsdp", None)),
        check_vma=False,
    )
```

profile of v0, /device:TPU:1, one launch (start us, length us, event | category | flops | bytes accessed | tf_op | source)
XLA Modules:
  0.0 1052.5 jit_solution(8933292455666120122)
XLA Ops:
  7.2 0.0 all-gather.4.cloned.1.call-start
  7.2 0.7 all-gather.4.cloned.1.call-update
  7.9 0.0 all-gather.6.cloned.1.call-start
  7.9 0.7 all-gather.6.cloned.1.call-update
  8.6 0.0 all-gather.8.cloned.1.call-start
  8.7 0.7 all-gather.8.cloned.1.call-update
  9.4 0.0 all-reduce.3.cloned.1.call-start
  9.4 0.6 fusion.25
  10.7 157.4 %all-gather.4.cloned.1.call-done = bf16[8192,256]{1,0:T(8,128)(2,1)} async-done(((bf16[128,256]{1,0:T(8,128)(2,1)}), bf16[8192,256]{1,0:T(8,128)(2,1)}) %all-gather.4.cloned.1.call-update) | async-done | bytes 4194320 | tf_op jit(solution)/shard_map/all_gather | solution.py:73
  168.1 148.8 %all-gather.6.cloned.1.call-done = bf16[8192,256]{1,0:T(8,128)(2,1)} async-done(((bf16[128,256]{1,0:T(8,128)(2,1)}), bf16[8192,256]{1,0:T(8,128)(2,1)}) %all-gather.6.cloned.1.call-update) | async-done | bytes 4194320 | tf_op jit(solution)/shard_map/all_gather | solution.py:74
  316.9 11.1 %conditional.1 = (f32[2,128]{1,0:T(2,128)S(1)}, f32[2,128,128]{1,2,0:T(8,128)S(1)}) conditional(s32[]{:T(128)} %convert_element_type.20, () %tuple.16, (s32[128]{0:T(128)S(1)}, bf16[128,256]{1,0:T(8,128)(2,1)}, bf16[8192,256]{1,0:T(8,128)(2,1)}, bf16[8192,256]{1,0:T(8,128)(2,1)}) %tuple.17), branch_computations={%region_1.0_spmd, %region_2.5_spmd} | conditional | flops 1093664512 | bytes 37952016 | solution.py:44
  316.9 0.7 iota_compare_fusion
  317.6 4.0 fusion.27
  321.6 4.2 fusion.3
  325.9 2.1 fusion.2
  328.0 0.0 copy-start.1
  328.0 0.0 copy-start
  328.0 128.6 %all-gather.8.cloned.1.call-done = bf16[256,3072]{0,1:T(8,128)(2,1)} async-done(((bf16[256,48]{0,1:T(8,128)(2,1)}), bf16[256,3072]{0,1:T(8,128)(2,1)}) %all-gather.8.cloned.1.call-update) | async-done | bytes 1572880 | tf_op jit(solution)/shard_map/all_gather | solution.py:87
  456.7 3.2 fusion.28
  459.9 0.0 all-reduce.3.cloned.1.call-update
  459.9 25.7 %all_gather.15 = bf16[3072,128]{1,0:T(8,128)(2,1)S(1)} all-gather(bf16[384,128]{1,0:T(8,128)(2,1)S(1)} %copy-done.1), channel_id=1, replica_groups=mesh['fsdp'=8,'ctx'=64] {'fsdp'}, dimensions={0}, use_global_device_ids=true | all-gather | bytes 884736 | tf_op jit(solution)/shard_map/all_gather | solution.py:92
  485.6 60.2 %all-reduce.3.cloned.1.call-done = f32[128,3072]{1,0:T(8,128)} async-done(((f32[128,3072]{1,0:T(8,128)}), f32[128,3072]{1,0:T(8,128)}) %all-reduce.3.cloned.1.call-update) | async-done | bytes 1572880 | tf_op jit(solution)/shard_map/psum | solution.py:90
  545.8 1.6 convert_add_fusion
  547.4 0.9 fusion.29
  548.3 8.0 collective-permute-start
  556.3 0.1 copy.19
  556.4 0.6 collective-permute-done
  557.0 0.1 negate_multiply_fusion
  557.1 0.1 maximum_multiply_fusion
  557.2 1.9 collective-permute-start.1
  559.1 0.7 reshape.46
  559.9 17.3 %all-to-all-start = ((f32[64,1,128]{2,1,0:T(1,128)}), f32[64,1,128]{2,1,0:T(1,128)S(1)}, u32[]{:S(2)}, u32[]{:S(2)}) async-start(f32[64,1,128]{2,1,0:T(1,128)} %reshape.46), calls=%async_computation | async-start | bytes 65536 | tf_op jit(solution)/shard_map/all_to_all | solution.py:110
  577.2 0.0 all-reduce.5.cloned.1.call-start
  577.2 0.0 collective-permute-done.1
  577.2 1.2 fusion.15
  578.4 0.0 all-reduce.5.cloned.1.call-update
  578.4 13.4 %all-to-all-done = f32[64,1,128]{2,1,0:T(1,128)S(1)} async-done(((f32[64,1,128]{2,1,0:T(1,128)}), f32[64,1,128]{2,1,0:T(1,128)S(1)}, u32[]{:S(2)}, u32[]{:S(2)}) %all-to-all-start) | async-done | bytes 32800 | tf_op jit(solution)/shard_map/all_to_all | solution.py:110
  591.9 0.5 broadcast.19
  592.4 0.7 reduce
  593.1 0.1 reshape.47
  593.2 0.1 rev.6
  593.4 0.1 reshape.48
  593.5 18.8 %all_to_all.10 = f32[64,1,128]{2,1,0:T(1,128)S(1)} all-to-all(f32[64,1,128]{2,1,0:T(1,128)S(1)} %reshape.48), channel_id=1, replica_groups=mesh['fsdp'=8,'ctx'=64] {'ctx'}, dimensions={0} | all-to-all | bytes 65536 | tf_op jit(solution)/shard_map/all_to_all | solution.py:110
  612.3 0.7 reduce.1
  613.0 0.1 reshape.49
  613.1 0.7 copy.20
  613.8 430.5 %all-reduce.5.cloned.1.call-done = f32[384,128]{1,0:T(8,128)} async-done(((f32[384,128]{1,0:T(8,128)}), f32[384,128]{1,0:T(8,128)}) %all-reduce.5.cloned.1.call-update) | async-done | bytes 196624 | tf_op jit(solution)/shard_map/psum | solution.py:106
  1044.3 1.6 copy.48
  (12 shorter events, 0.1 us)
Async XLA Ops:
  7.2 160.9 %all-gather.4.cloned.1.call-start = ((), (), s32[]{:S(2)}) async-start(), calls=%async_computation.2 | async-start | bytes 4259840 | tf_op jit(solution)/shard_map/all_gather | solution.py:73
  7.9 309.0 %all-gather.6.cloned.1.call-start = ((), (), s32[]{:S(2)}) async-start(), calls=%async_computation.3 | async-start | bytes 4259840 | tf_op jit(solution)/shard_map/all_gather | solution.py:74
  8.6 448.0 %all-gather.8.cloned.1.call-start = ((), (), s32[]{:S(2)}) async-start(), calls=%async_computation.4 | async-start | bytes 1597440 | tf_op jit(solution)/shard_map/all_gather | solution.py:87
  9.4 536.4 %all-reduce.3.cloned.1.call-start = ((), (), s32[]{:S(2)}) async-start(), calls=%async_computation.5 | async-start | bytes 3145728 | tf_op jit(solution)/shard_map/psum | solution.py:90
  328.0 131.9 %copy-start.1 = (bf16[384,128]{1,0:T(8,128)(2,1)S(1)}, bf16[384,128]{1,0:T(8,128)(2,1)}, u32[]{:S(2)}) copy-start(bf16[384,128]{1,0:T(8,128)(2,1)} %param.15) | copy-start | bytes 294916
  328.0 217.8 %copy-start = (bf16[128,3072]{1,0:T(8,128)(2,1)S(1)}, bf16[128,3072]{1,0:T(8,128)(2,1)}, u32[]{:S(2)}) copy-start(bf16[128,3072]{1,0:T(8,128)(2,1)} %param.10) | copy-start | bytes 2359300
  459.9 96.4 %copy-start.2 = (f32[128,64]{0,1:T(8,128)S(1)}, f32[128,64]{0,1:T(8,128)}, u32[]{:S(2)}) copy-start(f32[128,64]{0,1:T(8,128)} %param.9) | copy-start | bytes 98308
  548.3 8.7 collective-permute-start
  557.2 20.0 %collective-permute-start.1 = (f32[1,128]{1,0:T(1,128)S(1)}, f32[1,128]{1,0:T(1,128)S(1)}, u32[]{:S(2)}, u32[]{:S(2)}) collective-permute-start(f32[1,128]{1,0:T(1,128)S(1)} %slice.29), channel_id=1, source_target_pairs={{1,0},{2,1},{3,2},{4,3},{5,4},{6,5},{7,6},{8,7},{9,8},{10,9},{11,1... | collective-permute-start | bytes 1544 | tf_op jit(solution)/shard_map/ppermute | solution.py:12
  559.9 32.0 %all-to-all-start = ((f32[64,1,128]{2,1,0:T(1,128)}), f32[64,1,128]{2,1,0:T(1,128)S(1)}, u32[]{:S(2)}, u32[]{:S(2)}) async-start(f32[64,1,128]{2,1,0:T(1,128)} %reshape.46), calls=%async_computation | async-start | bytes 65536 | tf_op jit(solution)/shard_map/all_to_all | solution.py:110
  577.2 467.2 %all-reduce.5.cloned.1.call-start = ((), (), s32[]{:S(2)}) async-start(), calls=%async_computation.6 | async-start | bytes 393216 | tf_op jit(solution)/shard_map/psum | solution.py:106
Sparse Core Ops, SparseCore 0:
  11.3 156.7 all-gather.3
  171.4 145.4 all-gather.5
  320.2 136.4 all-gather.7
  460.0 85.7 all-reduce.2
  581.2 463.1 all-reduce.4
where the time goes:
time: 1050 us
  waiting for transfers between devices  942 us (90%)
  blocking collectives  44.5 us (4%)
  starting transfers between devices  27.4 us (3%)
  between operations  14.6 us (1%)
  matrix products  13.5 us (1%)
    psum x1, waiting for transfers between devices, shards(): head_grad = lax.psum(grad_part, 'ctx')  431 us
    all_gather x1, waiting for transfers between devices, shards(): lax.all_gather(key_rows, 'ctx', axis=0, tiled=True)  157 us
    all_gather x1, waiting for transfers between devices, shards(): lax.all_gather(value_rows, 'ctx', axis=0, tiled=True)  149 us
    all_gather x1, waiting for transfers between devices, shards(): lax.all_gather(w_mix, 'ctx', axis=1, tiled=True)  129 us
    psum x1, waiting for transfers between devices, shards(): mixed = lax.psum(mixed_part, 'fsdp')  60.2 us
    all_gather x1, blocking collectives, shards(): head_full = lax.all_gather(w_head, 'fsdp', axis=0, tiled=True)  25.7 us
  transfers between devices with their start and end apart: 8, of which 7 were waited for; matrix products, arithmetic and copies ran while one was open for 2% of the time, Pallas kernels for 0%

commit v1 on v0

v1 whole, which is shorter than its diff:
```python
import functools
import math

import jax
import jax.numpy as jnp
from jax import lax
from jax.experimental import pallas as pl
from jax.experimental.pallas import tpu as pltpu
from jax.sharding import PartitionSpec as P

HD = 128
MESH = pl.DeviceIdType.MESH
F32, BF16 = jnp.float32, jnp.bfloat16
NT_DIMS = (((1,), (1,)), ((), ()))
SCALE = HD**-0.5 * math.log2(math.e)


def remote(src, dst, send, recv, f, c):
    return pltpu.make_async_remote_copy(
        src_ref=src, dst_ref=dst, send_sem=send, recv_sem=recv, device_id=(f, c), device_id_type=MESH
    )


def greet(barrier, f, c):
    pl.semaphore_signal(barrier, inc=1, device_id=(f, c), device_id_type=MESH)


class Place:
    def __init__(self, F, C):
        self.F, self.C, self.Z = F, C, C // 4
        self.f, self.c = lax.axis_index("fsdp"), lax.axis_index("ctx")
        self.row = self.f // (F // 2)
        self.half = self.c // (C // 2)
        self.z = lax.rem(self.c, C // 2) // 2
        self.k = lax.rem(self.c, 2)
        self.sib = self.c + 1 - 2 * self.k
        self.mate = lax.rem(self.c + C // 2, C)

    def at(self, half, z, k):
        return half * (self.C // 2) + z * 2 + k

    def zrel(self, by):
        return lax.rem(self.z + by + self.Z, self.Z)


def dot_nt(a, b):
    return lax.dot_general(a, b, NT_DIMS, preferred_element_type=F32)


def split3(x):
    a = x.astype(BF16)
    rest = x - a.astype(F32)
    b = rest.astype(BF16)
    return a, b, (rest - b.astype(F32)).astype(BF16)


def attend_kernel(
    F, C, q_ref, k_ref, v_ref, w_ref, att_ref, wt_ref,
    kbuf, vbuf, wbuf, q2, m_s, l_s, acc_s, o_in, st_out, st_in, tbuf,
    ring_send, ring_recv, sib_send, sib_recv, w_send, w_recv, w2_send, w2_recv, ws_sem, q_sem, o_send, o_recv,
):
    p = Place(F, C)
    f, z, k, half, Z = p.f, p.z, p.k, p.half, p.Z
    steps, groups = Z // 2, F // 2
    per = Z // groups
    tok = q_ref.shape[0]
    wide = w_ref.shape[1]
    above, below = p.at(half, p.zrel(1), k), p.at(half, p.zrel(-1), k)

    barrier = pltpu.get_barrier_semaphore()
    for c in (above, below, p.sib, p.mate):
        greet(barrier, f, c)
    mine = p.row == half
    for g in range(groups):
        for h in range(2):
            fd, cd = half * groups + g, p.at(h, z, k)

            @pl.when(jnp.logical_not(jnp.logical_and(fd == f, cd == p.c)))
            def _():
                greet(barrier, fd, cd)

    for fs in range(F):
        cs = p.at(p.row, z, k)

        @pl.when(jnp.logical_not(jnp.logical_and(fs == f, cs == p.c)))
        def _():
            greet(barrier, fs, cs)

    kbuf[z, k] = k_ref[...]
    vbuf[z, k] = v_ref[...]
    wbuf[z] = w_ref[...]
    m_s[...] = jnp.full_like(m_s, -1e30)
    l_s[...] = jnp.zeros_like(l_s)
    acc_s[...] = jnp.zeros_like(acc_s)
    pl.semaphore_wait(barrier, 4 + 2 * F - 2 * mine.astype(jnp.int32))

    def buf(kind):
        return kbuf if kind % 2 == 0 else vbuf

    def origin(kind, s):
        return p.zrel(-s) if kind < 2 else p.zrel(s)

    def ring(kind, s, o):
        return remote(
            buf(kind).at[o, k], buf(kind).at[o, k], ring_send.at[kind, s], ring_recv.at[kind, s],
            f, above if kind < 2 else below,
        )

    def beside(kind, s, core):
        o = origin(kind, s)
        return remote(
            buf(kind).at[o, core], buf(kind).at[o, core], sib_send.at[kind, s], sib_recv.at[kind, s], f, p.sib
        )

    def wring(up, s, o):
        return remote(
            wbuf.at[o], wbuf.at[o], w_send.at[up, s], w_recv.at[up, s], f, above if up == 0 else below
        )

    for kind in (0, 2, 1, 3):
        ring(kind, 1, z).start()
    for up in (0, 1):
        wring(up, 1, z).start()
    for kind in (0, 1):
        beside(kind, 0, k).start()
    to_mate = remote(q_ref, q2, q_sem.at[0], q_sem.at[1], f, p.mate)

    @pl.when(half == 1)
    def _():
        to_mate.start()

    def fold(who, o, masked=False):
        for h in range(2):
            cols = slice(h * HD, (h + 1) * HD)
            q = (q_ref if who == 0 else q2)[:, cols]
            kk = kbuf[o, :, :, cols].reshape(2 * tok, HD)
            vv = vbuf[o, :, :, cols].reshape(2 * tok, HD)
            s = dot_nt(q, kk)
            if masked:
                row = k * tok + lax.broadcasted_iota(jnp.int32, s.shape, 0)
                s = jnp.where(lax.broadcasted_iota(jnp.int32, s.shape, 1) <= row, s, -1e30)
            s0, s1 = s[:, :tok], s[:, tok:]
            m_old = m_s[who, h]
            top = jnp.max(jnp.maximum(s0, s1), axis=1, keepdims=True)
            m_new = jnp.maximum(m_old, top)
            keep = jnp.exp2((m_old - m_new) * SCALE)
            p0 = jnp.exp2((s0 - m_new) * SCALE)
            p1 = jnp.exp2((s1 - m_new) * SCALE)
            m_s[who, h] = m_new
            l_s[who, h] = l_s[who, h] * keep + (p0 + p1)
            both = jnp.concatenate([p0.astype(BF16), p1.astype(BF16)], axis=1)
            acc_s[who, h] = acc_s[who, h] * keep + jnp.dot(both, vv, preferred_element_type=F32)

    def arrive(kind, s):
        o = origin(kind, s)
        ring(kind, s, o).wait_recv()
        last = steps if kind < 2 else steps - 1

        @pl.when(s < last)
        def _():
            ring(kind, s + 1, o).start()

        beside(kind, s, k).start()

    def w_arrive(up, s):
        o = p.zrel(-s) if up == 0 else p.zrel(s)
        wring(up, s, o).wait_recv()
        last = steps if up == 0 else steps - 1

        @pl.when(s < last)
        def _():
            wring(up, s + 1, o).start()

    def first_fold():
        beside(0, 0, 1 - k).wait_recv()
        beside(1, 0, 1 - k).wait_recv()

        @pl.when(half == 0)
        def _():
            to_mate.wait_recv()
            fold(1, z)

        fold(0, z, masked=True)

    def fold_step(s):
        for base in (0, 2):
            o = origin(base, s)
            beside(base, s, 1 - k).wait_recv()
            beside(base + 1, s, 1 - k).wait_recv()

            @pl.when(half == 0)
            def _():
                fold(1, o)

            seen = z >= s if base == 0 else z + s >= Z

            @pl.when(seen)
            def _():
                fold(0, o)

    def to_plane(g, h):
        return remote(
            wbuf.at[pl.ds(g * per, per)], wt_ref.at[:, k, :, pl.ds(pl.multiple_of(f * wide, wide), wide)],
            w2_send.at[g, h], w2_recv.at[f], half * groups + g, p.at(h, z, k),
        )

    def elsewhere(g, h):
        return jnp.logical_not(jnp.logical_and(half * groups + g == f, half == h))

    def spread_w():
        for g in range(groups):
            for h in range(2):

                @pl.when(elsewhere(g, h))
                def _():
                    to_plane(g, h).start()

        @pl.when(mine)
        def _():
            g = f - half * groups
            wt_ref[:, k, :, pl.ds(pl.multiple_of(f * wide, wide), wide)] = wbuf[pl.ds(g * per, per)]

    @pl.loop(1, steps + 1)
    def _(s):
        arrive(0, s)

        @pl.when(s < steps)
        def _():
            arrive(2, s)

        arrive(1, s)

        @pl.when(s < steps)
        def _():
            arrive(3, s)

        @pl.when(s <= steps // 2)
        def _():
            w_arrive(0, 2 * s - 1)
            w_arrive(1, 2 * s - 1)

        @pl.when(s == 1)
        def _():
            first_fold()

        @pl.when(s > 1)
        def _():
            fold_step(s - 1)

        @pl.when(s <= steps // 2)
        def _():
            w_arrive(0, 2 * s)

            @pl.when(2 * s < steps)
            def _():
                w_arrive(1, 2 * s)

        @pl.when(s == steps // 2)
        def _():
            spread_w()

    far = origin(0, steps)
    beside(0, steps, 1 - k).wait_recv()
    beside(1, steps, 1 - k).wait_recv()
    lane = lax.broadcasted_iota(jnp.int32, (tok, 128), 1)
    back = [
        remote(acc_s.at[1], o_in, o_send.at[0], o_recv.at[0], f, p.mate),
        remote(st_out, st_in, o_send.at[1], o_recv.at[1], f, p.mate),
    ]

    @pl.when(half == 0)
    def _():
        fold(1, far)
        back[0].start()
        stats = jnp.zeros((tok, 128), F32)
        for h in range(2):
            stats = jnp.where(lane == h, m_s[1, h], stats)
            stats = jnp.where(lane == 2 + h, jnp.sum(l_s[1, h], axis=1, keepdims=True), stats)
        st_out[...] = stats.T[:8]
        back[1].start()

    @pl.when(z >= steps)
    def _():
        fold(0, far)

    def from_plane(fs):
        return remote(
            wbuf.at[pl.ds(0, per)], wt_ref.at[:, k, :, pl.ds(fs * wide, wide)],
            w2_send.at[0, 0], w2_recv.at[fs], fs, p.at(p.row, z, k),
        )

    for fs in range(F):

        @pl.when(jnp.logical_not(jnp.logical_and(mine, fs == f)))
        def _():
            from_plane(fs).wait_recv()

    across = remote(wt_ref.at[:, k], wt_ref.at[:, k], ws_sem.at[0], ws_sem.at[1], f, p.sib)
    across.start()

    def store(h, acc, total):
        att_ref[:, h * HD : (h + 1) * HD] = (acc / total).astype(BF16)

    @pl.when(half == 0)
    def _():
        for h in range(2):
            store(h, acc_s[0, h], jnp.sum(l_s[0, h], axis=1, keepdims=True))

    @pl.when(half == 1)
    def _():
        back[0].wait_recv()
        back[1].wait_recv()
        tbuf[...] = jnp.zeros_like(tbuf)
        tbuf[:8] = st_in[...]
        stats = tbuf[...].T
        for h in range(2):
            m_a, l_a = m_s[0, h], jnp.sum(l_s[0, h], axis=1, keepdims=True)
            m_b = jnp.max(jnp.where(lane == h, stats, -3e38), axis=1, keepdims=True)
            l_b = jnp.sum(jnp.where(lane == 2 + h, stats, 0.0), axis=1, keepdims=True)
            m = jnp.maximum(m_a, m_b)
            e_a, e_b = jnp.exp2((m_a - m) * SCALE), jnp.exp2((m_b - m) * SCALE)
            store(h, acc_s[0, h] * e_a + o_in[h] * e_b, l_a * e_a + l_b * e_b)

    remote(wt_ref.at[:, 1 - k], wt_ref.at[:, 1 - k], ws_sem.at[0], ws_sem.at[1], f, p.sib).wait_recv()

    @pl.loop(1, steps + 1)
    def _(s):
        for kind in (0, 1):
            ring(kind, s, z).wait_send()
            beside(kind, s, k).wait_send()
        wring(0, s, z).wait_send()

        @pl.when(s < steps)
        def _():
            for kind in (2, 3):
                ring(kind, s, z).wait_send()
                beside(kind, s, k).wait_send()
            wring(1, s, z).wait_send()

    for kind in (0, 1):
        beside(kind, 0, k).wait_send()
    for g in range(groups):
        for h in range(2):

            @pl.when(elsewhere(g, h))
            def _():
                to_plane(g, h).wait_send()

    across.wait_send()

    @pl.when(half == 0)
    def _():
        back[0].wait_send()
        back[1].wait_send()

    @pl.when(half == 1)
    def _():
        to_mate.wait_send()


def attend(F, C, queries, key_rows, value_rows, w_t):
    tok, width = queries.shape
    cols, wide = w_t.shape
    Z = C // 4
    per = Z // (F // 2)
    n = Z // 2 + 1
    dma = pltpu.SemaphoreType.DMA
    vmem = pl.BlockSpec(memory_space=pltpu.VMEM)
    return pl.pallas_call(
        functools.partial(attend_kernel, F, C),
        out_shape=(
            jax.ShapeDtypeStruct((tok, width), BF16),
            jax.ShapeDtypeStruct((per, 2, cols, F * wide), BF16),
        ),
        in_specs=[vmem] * 4,
        out_specs=(vmem, vmem),
        scratch_shapes=[
            pltpu.VMEM((Z, 2, tok, width), BF16),
            pltpu.VMEM((Z, 2, tok, width), BF16),
            pltpu.VMEM((Z, cols, wide), BF16),
            pltpu.VMEM((tok, width), BF16),
            pltpu.VMEM((2, 2, tok, 128), F32),
            pltpu.VMEM((2, 2, tok, 128), F32),
            pltpu.VMEM((2, 2, tok, HD), F32),
            pltpu.VMEM((2, tok, HD), F32),
            pltpu.VMEM((8, tok), F32),
            pltpu.VMEM((8, tok), F32),
            pltpu.VMEM((128, tok), F32),
            dma((4, n)), dma((4, n)), dma((4, n)), dma((4, n)), dma((2, n)), dma((2, n)),
            dma((F // 2, 2)), dma((F,)), dma((2,)), dma((2,)), dma((2,)), dma((2,)),
        ],
        compiler_params=pltpu.CompilerParams(
            collective_id=0, has_side_effects=True, vmem_limit_bytes=40 * 1024 * 1024
        ),
        name="attend",
    )(queries, key_rows, value_rows, w_t)


def head_kernel(
    F, C, att_ref, wt_ref, stream_ref, wh_ref, lat_ref, flip_ref, hg_ref,
    attbuf, strm, edge_out, edge_in, lat128, pp, rs, pall, psum, flip_out, flip_in, last_out, last_in,
    part, cbuf, ybuf, ybuf_in, zbuf, rbuf, tile, full,
    strm_sem, att_send, att_recv, edge_sem, rs_send, rs_recv, ag_send, ag_recv, flip_sem, last_sem, core_sem, half_sem,
    zs_send, zs_recv, zg_send, zg_recv, half2_sem, core2_sem,
):
    p = Place(F, C)
    f, c, z, k, half, Z = p.f, p.c, p.z, p.k, p.half, p.Z
    tok, wide = att_ref.shape
    share = wh_ref.shape[0]
    chan = lat_ref.shape[1]
    reducers = zbuf.shape[0]
    prev, nxt = lax.rem(c + C - 1, C), lax.rem(c + 1, C)
    mirror, mirror2 = C - 1 - c, lax.rem(2 * C - 2 - c, C)
    own_last = mirror2 == c

    strm_copy = pltpu.make_async_copy(
        stream_ref.at[:, pl.ds(pl.multiple_of(f * share, 128), share)], strm, strm_sem.at[0]
    )
    strm_copy.start()

    barrier = pltpu.get_barrier_semaphore()

    @pl.loop(1, F)
    def _(r):
        greet(barrier, lax.rem(f + r, F), c)

    @pl.loop(1, Z)
    def _(r):
        greet(barrier, f, p.at(half, p.zrel(r), k))

    for other in (prev, nxt, p.sib, p.mate, mirror):
        greet(barrier, f, other)

    @pl.when(jnp.logical_not(own_last))
    def _():
        greet(barrier, f, mirror2)

    mine = pl.ds(pl.multiple_of(f * wide, wide), wide)
    attbuf[:, mine] = att_ref[...]
    lat128[...] = jnp.zeros_like(lat128)
    lat128[:, :chan] = lat_ref[...]
    edge_out[...] = lat128[:8]
    pl.semaphore_wait(barrier, (F - 1) + (Z - 1) + 6 - own_last.astype(jnp.int32))

    def att_copy(r):
        return remote(
            att_ref, attbuf.at[:, mine], att_send.at[r], att_recv.at[f], lax.rem(f + r, F), c
        )

    @pl.loop(1, F)
    def _(r):
        att_copy(r).start()

    edge = remote(edge_out, edge_in, edge_sem.at[0], edge_sem.at[1], f, prev)
    edge.start()

    strm_copy.wait()
    stream_t = strm[...].astype(F32).T
    wh_t = wh_ref[...].astype(F32).T.astype(BF16)
    edge.wait_recv()
    lat_rows = lat128[...]
    row = lax.broadcasted_iota(jnp.int32, lat_rows.shape, 0)
    lat_next = jnp.where(row == tok - 1, edge_in[0:1, :], pltpu.roll(lat_rows, tok - 1, 0)).T[:chan]

    @pl.loop(1, F)
    def _(r):
        fs = lax.rem(f + r, F)
        there = pl.ds(pl.multiple_of(fs * wide, wide), wide)
        remote(att_ref, attbuf.at[:, there], att_send.at[r], att_recv.at[fs], fs, c).wait_recv()

    resid = stream_t + dot_nt(wt_ref[...], attbuf[...])
    r_hi, r_mid, r_lo = split3(resid)
    partial = jnp.dot(wh_t, r_lo, preferred_element_type=F32)
    partial += jnp.dot(wh_t, r_mid, preferred_element_type=F32)
    partial += jnp.dot(wh_t, r_hi, preferred_element_type=F32)
    pp[...] = partial.reshape(pp.shape)

    @pl.loop(1, F)
    def _(r):
        to = lax.rem(f + r, F)
        remote(pp.at[to], rs.at[f], rs_send.at[r], rs_recv.at[f], to, c).start()

    rs[f] = pp[f]

    @pl.loop(1, F)
    def _(r):
        fs = lax.rem(f + r, F)
        remote(pp.at[fs], rs.at[fs], rs_send.at[r], rs_recv.at[fs], fs, c).wait_recv()

    psum[...] = jnp.sum(rs[...], axis=0)

    @pl.loop(1, F)
    def _(r):
        remote(psum, pall.at[f], ag_send.at[r], ag_recv.at[f], lax.rem(f + r, F), c).start()

    pall[f] = psum[...]

    @pl.loop(1, F)
    def _(r):
        fs = lax.rem(f + r, F)
        remote(psum, pall.at[fs], ag_send.at[r], ag_recv.at[fs], fs, c).wait_recv()

    pred = pall[...].reshape(2 * chan, tok)
    col = lax.broadcasted_iota(jnp.int32, (chan, tok), 1)
    final = jnp.logical_and(c == C - 1, col == tok - 1)
    shift = jnp.where(final, 0.0, pred[:chan])
    log_scale = jnp.where(final, 0.0, pred[chan:])
    inverse = jnp.exp(-log_scale)
    white = (lat_next - shift) * inverse
    loss_scale = float(tok * C) ** -0.5
    d_shift = jnp.where(final, 0.0, -white * inverse * loss_scale)
    d_log = jnp.where(final, 0.0, (1.0 - white * white) * loss_scale)
    d_hi, d_mid, d_lo = split3(jnp.concatenate([d_shift, d_log], axis=0))
    grad = dot_nt(r_hi, d_lo) + dot_nt(r_lo, d_hi) + dot_nt(r_mid, d_mid)
    grad += dot_nt(r_hi, d_mid) + dot_nt(r_mid, d_hi)
    grad += dot_nt(r_hi, d_hi)
    part[...] = grad.reshape(part.shape)

    core_copy = remote(part.at[1 - k], cbuf, core_sem.at[0], core_sem.at[1], f, p.sib)
    core_copy.start()

    r_i = lax.broadcasted_iota(jnp.int32, (tok, tok), 0)
    t_i = lax.broadcasted_iota(jnp.int32, (tok, tok), 1)
    swap = jnp.logical_or(t_i == tok - 2 - r_i, jnp.logical_and(r_i == tok - 1, t_i == tok - 1))
    swap = jnp.where(swap, 1.0, 0.0).astype(BF16)
    w_hi, w_mid, w_lo = split3(jnp.concatenate([white, white], axis=0))
    turned = dot_nt(swap, w_hi) + dot_nt(swap, w_mid) + dot_nt(swap, w_lo)
    low = lax.broadcasted_iota(jnp.int32, (tok // 2, 2 * chan), 1) < chan
    flip_out[...] = jnp.where(low, turned[: tok // 2], turned[tok // 2 :])
    last_out[...] = turned[tok - 8 :]
    flip_copy = remote(flip_out, flip_in, flip_sem.at[0], flip_sem.at[1], f, mirror)
    last_copy = remote(last_out, last_in, last_sem.at[0], last_sem.at[1], f, mirror2)

    core_copy.wait_recv()
    ybuf[...] = part[k] + cbuf[...]
    half_copy = remote(ybuf.at[1 - half], ybuf_in, half_sem.at[0], half_sem.at[1], f, p.mate)
    half_copy.start()
    flip_copy.start()

    @pl.when(own_last)
    def _():
        last_in[...] = last_out[...]

    @pl.when(jnp.logical_not(own_last))
    def _():
        last_copy.start()

    half_copy.wait_recv()
    zbuf[...] = ybuf[half].reshape(zbuf.shape) + ybuf_in[...].reshape(zbuf.shape)

    @pl.loop(1, Z)
    def _(r):
        to = p.zrel(r)

        @pl.when(to < reducers)
        def _():
            remote(zbuf.at[to], rbuf.at[z], zs_send.at[r], zs_recv.at[z], f, p.at(half, to, k)).start()

    @pl.when(z < reducers)
    def _():
        rbuf[z] = zbuf[z]

        @pl.loop(1, Z)
        def _(r):
            fs = p.zrel(r)
            remote(zbuf.at[0], rbuf.at[fs], zs_send.at[r], zs_recv.at[fs], f, p.at(half, fs, k)).wait_recv()

        tile[...] = jnp.sum(rbuf[...], axis=0)

        @pl.loop(1, Z)
        def _(r):
            remote(tile, full.at[k, half, z], zg_send.at[r], zg_recv.at[z], f, p.at(half, p.zrel(r), k)).start()

        full[k, half, z] = tile[...]

    @pl.loop(1, Z)
    def _(r):
        fs = p.zrel(r)

        @pl.when(fs < reducers)
        def _():
            remote(tile, full.at[k, half, fs], zg_send.at[r], zg_recv.at[fs], f, p.at(half, fs, k)).wait_recv()

    to_half = remote(full.at[k, half], full.at[k, half], half2_sem.at[0], half2_sem.at[1], f, p.mate)
    to_half.start()

    flip_copy.wait_recv()

    @pl.when(jnp.logical_not(own_last))
    def _():
        last_copy.wait_recv()

    got = flip_in[...]
    flip_ref[: tok // 2] = got[:, :chan]
    upper = pltpu.roll(got, chan, 1)[:, :chan]
    tail = lax.broadcasted_iota(jnp.int32, upper.shape, 0) == tok // 2 - 1
    flip_ref[tok // 2 :] = jnp.where(tail, last_in[7:8, :chan], upper)

    remote(full.at[k, 1 - half], full.at[k, 1 - half], half2_sem.at[0], half2_sem.at[1], f, p.mate).wait_recv()
    to_core = remote(full.at[k], full.at[k], core2_sem.at[0], core2_sem.at[1], f, p.sib)
    to_core.start()
    remote(full.at[1 - k], full.at[1 - k], core2_sem.at[0], core2_sem.at[1], f, p.sib).wait_recv()
    hg_ref[...] = full[...].reshape(hg_ref.shape)

    @pl.loop(1, F)
    def _(r):
        att_copy(r).wait_send()
        remote(pp.at[0], rs.at[0], rs_send.at[r], rs_recv.at[0], lax.rem(f + r, F), c).wait_send()
        remote(psum, pall.at[0], ag_send.at[r], ag_recv.at[0], lax.rem(f + r, F), c).wait_send()

    @pl.loop(1, Z)
    def _(r):
        to = p.zrel(r)

        @pl.when(to < reducers)
        def _():
            remote(zbuf.at[0], rbuf.at[0], zs_send.at[r], zs_recv.at[0], f, p.at(half, to, k)).wait_send()

        @pl.when(z < reducers)
        def _():
            remote(tile, full.at[0, 0, 0], zg_send.at[r], zg_recv.at[0], f, p.at(half, to, k)).wait_send()

    for copy in (edge, core_copy, half_copy, flip_copy, to_half, to_core):
        copy.wait_send()

    @pl.when(jnp.logical_not(own_last))
    def _():
        last_copy.wait_send()


def head(F, C, attended, wt, stream, w_head, latents):
    tok, wide = attended.shape
    share, chan2 = w_head.shape
    chan = latents.shape[1]
    Z = C // 4
    tiles = share // 4 // 8
    each = -(-tiles // Z)
    reducers = tiles // each
    dma = pltpu.SemaphoreType.DMA
    vmem = pl.BlockSpec(memory_space=pltpu.VMEM)
    block = (each * 8, chan2)
    return pl.pallas_call(
        functools.partial(head_kernel, F, C),
        out_shape=(
            jax.ShapeDtypeStruct((tok, chan), F32),
            jax.ShapeDtypeStruct((share, chan2), F32),
        ),
        in_specs=[vmem, vmem, pl.BlockSpec(memory_space=pl.ANY), vmem, vmem],
        out_specs=(vmem, vmem),
        scratch_shapes=[
            pltpu.VMEM((tok, F * wide), BF16),
            pltpu.VMEM((tok, share), BF16),
            pltpu.VMEM((8, 128), F32),
            pltpu.VMEM((8, 128), F32),
            pltpu.VMEM((tok, 128), F32),
            pltpu.VMEM((F, chan2 // F, tok), F32),
            pltpu.VMEM((F, chan2 // F, tok), F32),
            pltpu.VMEM((F, chan2 // F, tok), F32),
            pltpu.VMEM((chan2 // F, tok), F32),
            pltpu.VMEM((tok // 2, chan2), F32),
            pltpu.VMEM((tok // 2, chan2), F32),
            pltpu.VMEM((8, chan2), F32),
            pltpu.VMEM((8, chan2), F32),
            pltpu.VMEM((2, 2, reducers) + block, F32),
            pltpu.VMEM((2, reducers) + block, F32),
            pltpu.VMEM((2, reducers) + block, F32),
            pltpu.VMEM((reducers,) + block, F32),
            pltpu.VMEM((reducers,) + block, F32),
            pltpu.VMEM((Z,) + block, F32),
            pltpu.VMEM(block, F32),
            pltpu.VMEM((2, 2, reducers) + block, F32),
            dma((1,)), dma((F,)), dma((F,)), dma((2,)), dma((F,)), dma((F,)), dma((F,)), dma((F,)),
            dma((2,)), dma((2,)), dma((2,)), dma((2,)),
            dma((Z,)), dma((Z,)), dma((Z,)), dma((Z,)), dma((2,)), dma((2,)),
        ],
        compiler_params=pltpu.CompilerParams(
            collective_id=1, has_side_effects=True, vmem_limit_bytes=40 * 1024 * 1024
        ),
        name="head",
    )(attended, wt, stream, w_head, latents)


def shards(F, C, latents, stream, queries, key_rows, value_rows, w_mix, w_head):
    attended, wt = attend(F, C, queries, key_rows, value_rows, w_mix.T)
    wt = wt.reshape(-1, wt.shape[-1])
    return head(F, C, attended, wt, stream, w_head, latents)


def solution(mesh):
    return jax.shard_map(
        functools.partial(shards, mesh.shape["fsdp"], mesh.shape["ctx"]),
        mesh=mesh,
        in_specs=(
            P("ctx", None),
            P("ctx", None),
            P("ctx", "fsdp"),
            P("ctx", "fsdp"),
            P("ctx", "fsdp"),
            P("fsdp", "ctx"),
            P("fsdp", None),
        ),
        out_specs=(P("ctx", None), P("fsdp", None)),
        check_vma=False,
    )
```

time: 1050 us -> 126 us (0.12)
  waiting for transfers between devices: 942 us -> 0 us
  Pallas kernels: 0 us -> 117 us
  blocking collectives: 44.5 us -> 0 us
  starting transfers between devices: 27.4 us -> 0 us
  between operations: 14.6 us -> 0.67 us
  matrix products: 13.5 us -> 0 us
    psum x2 -> x0, waiting for transfers between devices: 491 us -> none  [the longest x1 431 us: shards(): head_grad = lax.psum(grad_part, 'ctx')]
    all_gather x3 -> x0, waiting for transfers between devices: 435 us -> none  [the longest x1 157 us: shards(): lax.all_gather(key_rows, 'ctx', axis=0, tiled=True)]
    pallas_call x0 -> x2, Pallas kernels: none -> 117 us  [the longest x1 62.8 us: attend(): pl.pallas_call(functools.partial(attend_kernel, F, C), out_shape=(jax.Sha...]
    all_gather x1 -> x0, blocking collectives: 25.7 us -> none  [shards(): head_full = lax.all_gather(w_head, 'fsdp', axis=0, tiled=True)]
    all_to_all x1 -> x0, blocking collectives: 18.8 us -> none  [mirror_step(): lax.all_to_all(pieces, 'ctx', split_axis=0, concat_axis=0, tiled=True)]
    all_to_all x1 -> x0, starting transfers between devices: 17.3 us -> none  [mirror_step(): lax.all_to_all(pieces, 'ctx', split_axis=0, concat_axis=0, tiled=True)]
    all_to_all x1 -> x0, waiting for transfers between devices: 13.4 us -> none  [mirror_step(): lax.all_to_all(pieces, 'ctx', split_axis=0, concat_axis=0, tiled=True)]
  transfers between devices with their start and end apart: 8 -> 0, of which waited for: 7 -> 0; matrix products, arithmetic and copies ran while one was open for 2% -> 0% of each run, Pallas kernels for 0% -> 0%
where the time goes in v1:
time: 126 us; the launch traced here: 125 us
  Pallas kernels  117 us (93%)
  local copies, waits for them, and re-layouts  7.5 us (6%)
    pallas_call x1, Pallas kernels, attend(): pl.pallas_call(functools.partial(attend_kernel, F, C), out_shape=(jax.Sha...  62.8 us
    pallas_call x1, Pallas kernels, head(): pl.pallas_call(functools.partial(head_kernel, F, C), out_shape=(jax.Shape...  54.4 us
    unnamed x14, local copies, waits for them, and re-layouts  6.8 us

profile of v1, /device:TPU:1, one launch (start us, length us, event | category | flops | bytes accessed | tf_op | source)
XLA Modules:
  0.0 125.4 jit_solution(7978399528909908666)
XLA Ops:
  0.6 0.8 copy.9.lat_ref
  1.5 0.0 copy-start.2
  1.5 0.8 copy-done.2
  2.3 0.0 copy-start.3
  2.3 0.8 copy-done.3
  3.2 0.0 copy-start.4
  3.2 0.8 copy-done.4
  4.0 0.0 copy-start.5
  4.0 0.7 copy-done.5
  4.7 62.8 %attend.1 = (bf16[128,256]{1,0:T(8,128)(2,1)S(1)}, bf16[4,2,48,2048]{3,2,1,0:T(8,128)(2,1)S(1)}) custom-call(bf16[128,256]{1,0:T(8,128)(2,1)S(1)} %copy-done.2, bf16[128,256]{1,0:T(8,128)(2,1)S(1)} %copy-done.3, bf16[128,256]{1,0:T(8,128)(2,1)S(1)} %copy-done.4, bf16[48,256]{1,0:T(8,128)(2,1)S(1)} %bitcast.3), custom_call_target="tpu_custom_call" | custom-call | tf_op jit(solution)/shard_map/attend/pallas_call | solution.py:369
  67.6 0.0 copy-start
  67.6 1.1 copy-done
  68.7 0.0 copy-start.1
  68.7 0.9 copy-done.1
  69.6 54.4 %head.1 = (f32[128,64]{1,0:T(8,128)S(1)}, f32[384,128]{1,0:T(8,128)S(1)}) custom-call(bf16[128,256]{1,0:T(8,128)(2,1)S(1)} %get-tuple-element.4.att_ref, bf16[384,2048]{1,0:T(8,128)(2,1)S(1)} %bitcast.2, bf16[128,3072]{1,0:T(8,128)(2,1)S(1)} %copy-done, bf16[384,128]{1,0:T(8,128)(2,1)S(1)} %copy-done.1, f32[128,64]{1,0:T(8,128)S(1)} %copy.9.lat_ref), custom_call_target="tpu_custom_call" | custom-call | tf_op jit(solution)/shard_map/head/pallas_call | solution.py:642
  124.1 0.7 copy.10
  124.8 0.7 copy.12
Async XLA Ops:
  1.5 0.8 copy-start.2
  2.3 0.8 copy-start.3
  3.2 0.8 copy-start.4
  4.0 0.7 copy-start.5
  67.6 1.1 copy-start
  68.7 0.9 copy-start.1

commit v2 on v1

v2 whole, which is shorter than its diff:
```python
import functools
import math

import jax
import jax.numpy as jnp
from jax import lax
from jax.experimental import pallas as pl
from jax.experimental.pallas import tpu as pltpu
from jax.sharding import PartitionSpec as P

HD = 128
MESH = pl.DeviceIdType.MESH
F32, BF16 = jnp.float32, jnp.bfloat16
NT_DIMS = (((1,), (1,)), ((), ()))
SCALE = HD**-0.5 * math.log2(math.e)


def remote(src, dst, send, recv, f, c):
    return pltpu.make_async_remote_copy(
        src_ref=src, dst_ref=dst, send_sem=send, recv_sem=recv, device_id=(f, c), device_id_type=MESH
    )


def greet(barrier, f, c):
    pl.semaphore_signal(barrier, inc=1, device_id=(f, c), device_id_type=MESH)


class Place:
    def __init__(self, F, C):
        self.F, self.C, self.Z = F, C, C // 4
        self.f, self.c = lax.axis_index("fsdp"), lax.axis_index("ctx")
        self.row = self.f // (F // 2)
        self.half = self.c // (C // 2)
        self.z = lax.rem(self.c, C // 2) // 2
        self.k = lax.rem(self.c, 2)
        self.sib = self.c + 1 - 2 * self.k
        self.mate = lax.rem(self.c + C // 2, C)
        self.prev, self.next = lax.rem(self.c + C - 1, C), lax.rem(self.c + 1, C)

    def at(self, half, z, k):
        return half * (self.C // 2) + z * 2 + k

    def plane(self, r):
        i = lax.rem(self.half * self.F + self.f + r, 2 * self.F)
        return lax.rem(i, self.F), self.at(i // self.F, self.z, self.k)

    def zrel(self, by):
        return lax.rem(self.z + by + self.Z, self.Z)


def dot_nt(a, b):
    return lax.dot_general(a, b, NT_DIMS, preferred_element_type=F32)


def split3(x):
    a = x.astype(BF16)
    rest = x - a.astype(F32)
    b = rest.astype(BF16)
    return a, b, (rest - b.astype(F32)).astype(BF16)


def entry(p, q_ref, k_ref, v_ref, w_ref, kbuf, vbuf, wbuf, qbuf, in_sem):
    z, k = p.z, p.k
    loads = [
        pltpu.make_async_copy(k_ref, kbuf.at[z, k], in_sem.at[0]),
        pltpu.make_async_copy(v_ref, vbuf.at[z, k], in_sem.at[1]),
        pltpu.make_async_copy(w_ref, wbuf.at[z], in_sem.at[2]),
        pltpu.make_async_copy(q_ref, qbuf, in_sem.at[3]),
    ]
    for load in loads:
        load.start()
    barrier = pltpu.get_barrier_semaphore()
    for c in (p.at(p.half, p.zrel(1), k), p.at(p.half, p.zrel(-1), k), p.sib, p.prev, p.next):
        greet(barrier, p.f, c)
    for r in (2, -2):
        greet(barrier, p.f, p.at(p.half, p.zrel(r), k))

    @pl.loop(1, 2 * p.F)
    def _(r):
        greet(barrier, *p.plane(r))

    for load in loads:
        load.wait()
    pl.semaphore_wait(barrier, 7 + 2 * p.F - 1)


class Weights:
    def __init__(
        self, p, wbuf, whv, stream, sp, mp, m_in, m_half, m_in2, mall,
        wh_send, wh_recv, whs_sem, ms_sem, mm_sem, mg_send, mg_recv, mx_sem,
    ):
        self.p, self.wbuf, self.whv, self.stream, self.sp = p, wbuf, whv, stream, sp
        self.mp, self.m_in, self.m_half, self.m_in2, self.mall = mp, m_in, m_half, m_in2, mall
        self.wh_sems, self.mg_sems = (wh_send, wh_recv), (mg_send, mg_recv)
        f, k = p.f, p.k
        self.whs_sem, self.mx_sem = whs_sem, mx_sem
        self.to_sib = remote(mp.at[1 - k], m_in, ms_sem.at[0], ms_sem.at[1], f, p.sib)
        self.to_mate = remote(m_half, m_in2, mm_sem.at[0], mm_sem.at[1], f, p.mate)

    def own(self, fs):
        groups = self.p.F // 2
        per = self.p.Z // groups
        return fs // groups, lax.rem(fs, groups) * per, per

    def rows(self, fs, core):
        h, at, per = self.own(fs)
        return self.whv.at[h, pl.ds(at + core * (per // 2), per // 2)]

    def head_copy(self, r, fs):
        p = self.p
        send, recv = self.wh_sems
        return remote(self.rows(fs, p.k), self.rows(fs, p.k), send.at[r], recv.at[fs], lax.rem(p.f + r, p.F), p.c)

    def beside(self, core, fs):
        return remote(
            self.rows(fs, core), self.rows(fs, core), self.whs_sem.at[0, fs], self.whs_sem.at[1, fs], self.p.f, self.p.sib
        )

    def start(self):
        @pl.loop(1, self.p.F)
        def _(r):
            self.head_copy(r, self.p.f).start()

    def share(self):
        p = self.p

        @pl.loop(1, p.F)
        def _(r):
            fs = lax.rem(p.f + r, p.F)
            self.head_copy(r, fs).wait_recv()
            self.beside(p.k, fs).start()

    def partial(self):
        p = self.p

        @pl.loop(1, p.F)
        def _(r):
            self.beside(1 - p.k, lax.rem(p.f + r, p.F)).wait_recv()

        width = self.wbuf.shape[2]
        rows = self.whv[p.half, :, p.k].reshape(-1, 128)
        pieces = self.wbuf[...].reshape(-1, width)
        out = jnp.dot(rows.astype(F32).T.astype(BF16), pieces, preferred_element_type=F32)
        self.mp[...] = out.reshape(self.mp.shape)
        self.to_sib.start()
        self.sp[...] = jnp.dot(self.stream[...], self.whv[...].reshape(-1, 128), preferred_element_type=F32).T

    def halves(self):
        self.to_sib.wait_recv()
        self.m_half[...] = self.mp[self.p.k] + self.m_in[...]
        self.to_mate.start()

    def lanes(self, fs):
        width = self.mp.shape[2]
        return pl.ds(pl.multiple_of(fs * width, width), width)

    def all_copy(self, r, fs):
        p = self.p
        send, recv = self.mg_sems
        dst = self.mall.at[p.k, :, self.lanes(fs)]
        return remote(dst, dst, send.at[r], recv.at[fs], lax.rem(p.f + r, p.F), p.c)

    def gather(self):
        p = self.p
        self.to_mate.wait_recv()
        self.mall[p.k, :, self.lanes(p.f)] = self.m_half[...] + self.m_in2[...]

        @pl.loop(1, p.F)
        def _(r):
            self.all_copy(r, p.f).start()

    def across(self, core):
        return remote(self.mall.at[core], self.mall.at[core], self.mx_sem.at[0], self.mx_sem.at[1], self.p.f, self.p.sib)

    def finish(self):
        p = self.p

        @pl.loop(1, p.F)
        def _(r):
            self.all_copy(r, lax.rem(p.f + r, p.F)).wait_recv()

        self.across(p.k).start()
        self.across(1 - p.k).wait_recv()

    def drain(self):
        p = self.p

        @pl.loop(1, p.F)
        def _(r):
            self.head_copy(r, p.f).wait_send()
            self.beside(p.k, lax.rem(p.f + r, p.F)).wait_send()
            self.all_copy(r, p.f).wait_send()

        self.to_sib.wait_send()
        self.to_mate.wait_send()
        self.across(p.k).wait_send()


def attend_phase(
    p, weights, q_ref, kbuf, vbuf, wbuf, q2, m_s, l_s, acc_s, o_in, st_out, st_in, tbuf, att_ref, wt_ref,
    ring_send, ring_recv, sib_send, sib_recv, w_send, w_recv, w2_send, w2_recv, ws_sem, q_sem, o_send, o_recv,
):
    F = p.F
    f, z, k, half, Z = p.f, p.z, p.k, p.half, p.Z
    steps, groups = Z // 2, F // 2
    per = Z // groups
    tok = q_ref.shape[0]
    wide = wbuf.shape[2]
    above, below = p.at(half, p.zrel(1), k), p.at(half, p.zrel(-1), k)
    mine = p.row == half

    m_s[...] = jnp.full_like(m_s, -1e30)
    l_s[...] = jnp.zeros_like(l_s)
    acc_s[...] = jnp.zeros_like(acc_s)

    def buf(kind):
        return kbuf if kind % 2 == 0 else vbuf

    def origin(kind, s):
        return p.zrel(-s) if kind < 2 else p.zrel(s)

    def ring(kind, s, o):
        return remote(
            buf(kind).at[o, k], buf(kind).at[o, k], ring_send.at[kind, s], ring_recv.at[kind, s],
            f, above if kind < 2 else below,
        )

    def beside(kind, s, core):
        o = origin(kind, s)
        return remote(
            buf(kind).at[o, core], buf(kind).at[o, core], sib_send.at[kind, s], sib_recv.at[kind, s], f, p.sib
        )

    def wring(up, dist, o):
        by = 2 - dist % 2 if isinstance(dist, int) else 2 - lax.rem(dist, 2)
        to = p.zrel(by) if up == 0 else p.zrel(-by)
        return remote(
            wbuf.at[o], wbuf.at[o], w_send.at[up, dist], w_recv.at[up, dist], f, p.at(half, to, k)
        )

    for kind in (0, 2, 1, 3):
        ring(kind, 1, z).start()
    for up in (0, 1):
        wring(up, 1, z).start()
        wring(up, 2, z).start()
    for kind in (0, 1):
        beside(kind, 0, k).start()
    to_mate = remote(q_ref, q2, q_sem.at[0], q_sem.at[1], f, p.mate)

    @pl.when(half == 1)
    def _():
        to_mate.start()

    weights.start()

    def fold(who, o, masked=False):
        for h in range(2):
            cols = slice(h * HD, (h + 1) * HD)
            q = (q_ref if who == 0 else q2)[:, cols]
            kk = kbuf[o, :, :, cols].reshape(2 * tok, HD)
            vv = vbuf[o, :, :, cols].reshape(2 * tok, HD)
            s = dot_nt(q, kk)
            if masked:
                row = k * tok + lax.broadcasted_iota(jnp.int32, s.shape, 0)
                s = jnp.where(lax.broadcasted_iota(jnp.int32, s.shape, 1) <= row, s, -1e30)
            s0, s1 = s[:, :tok], s[:, tok:]
            m_old = m_s[who, h]
            top = jnp.max(jnp.maximum(s0, s1), axis=1, keepdims=True)
            m_new = jnp.maximum(m_old, top)
            keep = jnp.exp2((m_old - m_new) * SCALE)
            p0 = jnp.exp2((s0 - m_new) * SCALE)
            p1 = jnp.exp2((s1 - m_new) * SCALE)
            m_s[who, h] = m_new
            l_s[who, h] = l_s[who, h] * keep + (p0 + p1)
            both = jnp.concatenate([p0.astype(BF16), p1.astype(BF16)], axis=1)
            acc_s[who, h] = acc_s[who, h] * keep + jnp.dot(both, vv, preferred_element_type=F32)

    def arrive(kind, s):
        o = origin(kind, s)
        ring(kind, s, o).wait_recv()
        last = steps if kind < 2 else steps - 1

        @pl.when(s < last)
        def _():
            ring(kind, s + 1, o).start()

        beside(kind, s, k).start()

    def w_origin(up, dist):
        return p.zrel(-dist) if up == 0 else p.zrel(dist)

    def w_arrive(s):
        for up in (0, 1):
            last = steps if up == 0 else steps - 1
            o = w_origin(up, 2 * s - 1)
            wring(up, 2 * s - 1, o).wait_recv()
            to_plane(o)

            @pl.when(2 * s <= last)
            def _():
                o = w_origin(up, 2 * s)
                wring(up, 2 * s, o).wait_recv()

                @pl.when(2 * s + 1 <= last)
                def _():
                    wring(up, 2 * s + 1, o).start()

                @pl.when(2 * s + 2 <= last)
                def _():
                    wring(up, 2 * s + 2, o).start()

                to_plane(o)

    def plane_copy(o, h):
        return remote(
            wbuf.at[o], wt_ref.at[lax.rem(o, per), k, :, pl.ds(pl.multiple_of(f * wide, wide), wide)],
            w2_send.at[o, h], w2_recv.at[f], half * groups + o // per, p.at(h, z, k),
        )

    def is_self(o, h):
        return jnp.logical_and(half * groups + o // per == f, half == h)

    def to_plane(o):
        for h in range(2):

            @pl.when(jnp.logical_not(is_self(o, h)))
            def _():
                plane_copy(o, h).start()

            @pl.when(is_self(o, h))
            def _():
                wt_ref[lax.rem(o, per), k, :, pl.ds(pl.multiple_of(f * wide, wide), wide)] = wbuf[o]

    def first_fold():
        beside(0, 0, 1 - k).wait_recv()
        beside(1, 0, 1 - k).wait_recv()

        @pl.when(half == 0)
        def _():
            to_mate.wait_recv()
            fold(1, z)

        fold(0, z, masked=True)

    def fold_step(s):
        for base in (0, 2):
            o = origin(base, s)
            beside(base, s, 1 - k).wait_recv()
            beside(base + 1, s, 1 - k).wait_recv()

            @pl.when(half == 0)
            def _():
                fold(1, o)

            seen = z >= s if base == 0 else z + s >= Z

            @pl.when(seen)
            def _():
                fold(0, o)

    to_plane(z)

    def from_plane(fs):
        return remote(
            wbuf.at[pl.ds(0, per)], wt_ref.at[:, k, :, pl.ds(fs * wide, wide)],
            w2_send.at[0, 0], w2_recv.at[fs], fs, p.at(p.row, z, k),
        )

    across = remote(wt_ref.at[:, k], wt_ref.at[:, k], ws_sem.at[0], ws_sem.at[1], f, p.sib)

    def collect():
        for fs in range(F):

            @pl.when(jnp.logical_not(jnp.logical_and(mine, fs == f)))
            def _():
                from_plane(fs).wait_recv()

        across.start()

    @pl.loop(1, steps + 1)
    def _(s):
        arrive(0, s)

        @pl.when(s < steps)
        def _():
            arrive(2, s)

        arrive(1, s)

        @pl.when(s < steps)
        def _():
            arrive(3, s)

        @pl.when(s <= steps // 2)
        def _():
            w_arrive(s)

        @pl.when(s == 3)
        def _():
            weights.share()

        @pl.when(s == steps // 2)
        def _():
            weights.partial()

        @pl.when(s == steps // 2 + 1)
        def _():
            weights.halves()

        @pl.when(s == steps - 1)
        def _():
            weights.gather()
            collect()

        @pl.when(s == 1)
        def _():
            first_fold()

        @pl.when(s > 1)
        def _():
            fold_step(s - 1)

    far = origin(0, steps)
    beside(0, steps, 1 - k).wait_recv()
    beside(1, steps, 1 - k).wait_recv()
    lane = lax.broadcasted_iota(jnp.int32, (tok, 128), 1)
    back = [
        remote(acc_s.at[1], o_in, o_send.at[0], o_recv.at[0], f, p.mate),
        remote(st_out, st_in, o_send.at[1], o_recv.at[1], f, p.mate),
    ]

    @pl.when(half == 0)
    def _():
        fold(1, far)
        back[0].start()
        stats = jnp.zeros((tok, 128), F32)
        for h in range(2):
            stats = jnp.where(lane == h, m_s[1, h], stats)
            stats = jnp.where(lane == 2 + h, jnp.sum(l_s[1, h], axis=1, keepdims=True), stats)
        st_out[...] = stats.T[:8]
        back[1].start()

    @pl.when(z >= steps)
    def _():
        fold(0, far)

    def store(h, acc, total):
        att_ref[:, h * HD : (h + 1) * HD] = (acc / total).astype(BF16)

    @pl.when(half == 0)
    def _():
        for h in range(2):
            store(h, acc_s[0, h], jnp.sum(l_s[0, h], axis=1, keepdims=True))

    @pl.when(half == 1)
    def _():
        back[0].wait_recv()
        back[1].wait_recv()
        tbuf[...] = jnp.zeros_like(tbuf)
        tbuf[:8] = st_in[...]
        stats = tbuf[...].T
        for h in range(2):
            m_a, l_a = m_s[0, h], jnp.sum(l_s[0, h], axis=1, keepdims=True)
            m_b = jnp.max(jnp.where(lane == h, stats, -3e38), axis=1, keepdims=True)
            l_b = jnp.sum(jnp.where(lane == 2 + h, stats, 0.0), axis=1, keepdims=True)
            m = jnp.maximum(m_a, m_b)
            e_a, e_b = jnp.exp2((m_a - m) * SCALE), jnp.exp2((m_b - m) * SCALE)
            store(h, acc_s[0, h] * e_a + o_in[h] * e_b, l_a * e_a + l_b * e_b)

    def early():
        weights.finish()
        remote(wt_ref.at[:, 1 - k], wt_ref.at[:, 1 - k], ws_sem.at[0], ws_sem.at[1], f, p.sib).wait_recv()

    def drain():
        attend_drain(p, ring, beside, wring, plane_copy, is_self, across, back, to_mate)

    return early, drain


def attend_drain(p, ring, beside, wring, plane_copy, is_self, across, back, to_mate):
    z, k, half, steps = p.z, p.k, p.half, p.Z // 2

    @pl.loop(1, steps + 1)
    def _(s):
        for kind in (0, 1):
            ring(kind, s, z).wait_send()
            beside(kind, s, k).wait_send()
        wring(0, s, z).wait_send()

        @pl.when(s < steps)
        def _():
            for kind in (2, 3):
                ring(kind, s, z).wait_send()
                beside(kind, s, k).wait_send()
            wring(1, s, z).wait_send()

    for kind in (0, 1):
        beside(kind, 0, k).wait_send()

    @pl.loop(0, p.Z)
    def _(o):
        for h in range(2):

            @pl.when(jnp.logical_not(is_self(o, h)))
            def _():
                plane_copy(o, h).wait_send()

    across.wait_send()

    @pl.when(half == 0)
    def _():
        back[0].wait_send()
        back[1].wait_send()

    @pl.when(half == 1)
    def _():
        to_mate.wait_send()


def head_phase(
    p, early, att_ref, wt_ref, stream, sp, mall, lat_ref, flip_ref, hg_ref,
    attbuf, edge_out, edge_in, flip_out, flip_in, last_out, last_in, part, cbuf, zbuf, rbuf, tile, full,
    att_send, att_recv, edge_sem, flip_sem, last_sem, core_sem, zs_send, zs_recv, zg_send, zg_recv, core2_sem,
):
    F, C = p.F, p.C
    f, c, z, k, half, Z = p.f, p.c, p.z, p.k, p.half, p.Z
    tok, wide = att_ref.shape
    chan = lat_ref.shape[0]
    reducers = zbuf.shape[0]
    mirror, mirror2 = C - 1 - c, lax.rem(2 * C - 2 - c, C)
    own_last = mirror2 == c
    lane = lax.broadcasted_iota(jnp.int32, (chan, tok), 1)

    def as_column(row):
        return jnp.broadcast_to(row, (tok, 128)).T

    mine = pl.ds(pl.multiple_of(f * wide, wide), wide)
    attbuf[:, mine] = att_ref[...]

    def att_copy(r):
        return remote(
            att_ref, attbuf.at[:, mine], att_send.at[r], att_recv.at[f], lax.rem(f + r, F), c
        )

    @pl.loop(1, F)
    def _(r):
        att_copy(r).start()

    lat_t = lat_ref[...]
    edge_out[...] = jnp.concatenate([lat_t, lat_t], axis=0).T[:8]
    edge = remote(edge_out, edge_in, edge_sem.at[0], edge_sem.at[1], f, p.prev)
    edge.start()
    share = hg_ref.shape[0]
    stream_t = stream[:, pl.ds(pl.multiple_of(f * share, 128), share)].astype(F32).T
    early()
    m_all = split3(mall[...].reshape(2 * chan, F * wide))
    edge.wait_recv()
    lat_next = jnp.where(lane == tok - 1, as_column(edge_in[0:1])[:chan], pltpu.roll(lat_t, tok - 1, 1))

    @pl.loop(1, F)
    def _(r):
        fs = lax.rem(f + r, F)
        there = pl.ds(pl.multiple_of(fs * wide, wide), wide)
        remote(att_ref, attbuf.at[:, there], att_send.at[r], att_recv.at[fs], fs, c).wait_recv()

    heads = attbuf[...]
    pred = sp[...] + (dot_nt(m_all[2], heads) + dot_nt(m_all[1], heads) + dot_nt(m_all[0], heads))
    resid = stream_t + dot_nt(wt_ref[...].reshape(share, F * wide), heads)
    r_hi, r_mid, r_lo = split3(resid)
    final = jnp.logical_and(c == C - 1, lane == tok - 1)
    shift = jnp.where(final, 0.0, pred[:chan])
    log_scale = jnp.where(final, 0.0, pred[chan:])
    inverse = jnp.exp(-log_scale)
    white = (lat_next - shift) * inverse
    loss_scale = float(tok * C) ** -0.5
    d_shift = jnp.where(final, 0.0, -white * inverse * loss_scale)
    d_log = jnp.where(final, 0.0, (1.0 - white * white) * loss_scale)
    d_hi, d_mid, d_lo = split3(jnp.concatenate([d_shift, d_log], axis=0))
    grad = dot_nt(r_hi, d_lo) + dot_nt(r_lo, d_hi) + dot_nt(r_mid, d_mid)
    grad += dot_nt(r_hi, d_mid) + dot_nt(r_mid, d_hi)
    grad += dot_nt(r_hi, d_hi)
    part[...] = grad.reshape(part.shape)

    core_copy = remote(part.at[1 - k], cbuf, core_sem.at[0], core_sem.at[1], f, p.sib)
    core_copy.start()

    t_i = lax.broadcasted_iota(jnp.int32, (tok, tok), 0)
    r_i = lax.broadcasted_iota(jnp.int32, (tok, tok), 1)
    swap = jnp.where(t_i == tok - 2 - r_i, 1.0, 0.0).astype(BF16)
    w_hi, w_mid, w_lo = split3(white)
    turned = jnp.dot(w_hi, swap, preferred_element_type=F32) + jnp.dot(w_mid, swap, preferred_element_type=F32)
    flip_out[...] = turned + jnp.dot(w_lo, swap, preferred_element_type=F32)
    last_out[...] = jnp.concatenate([white, white], axis=0).T[tok - 8 :]
    flip_copy = remote(flip_out, flip_in, flip_sem.at[0], flip_sem.at[1], f, mirror)
    last_copy = remote(last_out, last_in, last_sem.at[0], last_sem.at[1], f, mirror2)

    core_copy.wait_recv()
    zbuf[...] = part[k] + cbuf[...]
    ranks = 2 * Z
    me = half * Z + z

    def rank(r):
        i = lax.rem(me + r, ranks)
        return i, p.at(i // Z, lax.rem(i, Z), k)

    @pl.loop(1, ranks)
    def _(r):
        to, there = rank(r)

        @pl.when(to < reducers)
        def _():
            remote(zbuf.at[to], rbuf.at[me], zs_send.at[r], zs_recv.at[me], f, there).start()

    flip_copy.start()

    @pl.when(own_last)
    def _():
        last_in[...] = last_out[...]

    @pl.when(jnp.logical_not(own_last))
    def _():
        last_copy.start()

    @pl.when(me < reducers)
    def _():
        rbuf[me] = zbuf[me]

        @pl.loop(1, ranks)
        def _(r):
            i, there = rank(r)
            remote(zbuf.at[0], rbuf.at[i], zs_send.at[r], zs_recv.at[i], f, there).wait_recv()

        tile[...] = jnp.sum(rbuf[...], axis=0)

        @pl.loop(1, ranks)
        def _(r):
            remote(tile, full.at[k, me], zg_send.at[r], zg_recv.at[me], f, rank(r)[1]).start()

        full[k, me] = tile[...]

    flip_copy.wait_recv()

    @pl.when(jnp.logical_not(own_last))
    def _():
        last_copy.wait_recv()

    flip_ref[...] = jnp.where(lane == tok - 1, as_column(last_in[7:8])[:chan], flip_in[...])

    @pl.loop(1, ranks)
    def _(r):
        i, there = rank(r)

        @pl.when(i < reducers)
        def _():
            remote(tile, full.at[k, i], zg_send.at[r], zg_recv.at[i], f, there).wait_recv()

    to_core = remote(full.at[k], full.at[k], core2_sem.at[0], core2_sem.at[1], f, p.sib)
    to_core.start()
    remote(full.at[1 - k], full.at[1 - k], core2_sem.at[0], core2_sem.at[1], f, p.sib).wait_recv()
    hg_ref[...] = full[...].reshape(hg_ref.shape)

    @pl.loop(1, F)
    def _(r):
        att_copy(r).wait_send()

    @pl.loop(1, ranks)
    def _(r):
        i, there = rank(r)

        @pl.when(i < reducers)
        def _():
            remote(zbuf.at[0], rbuf.at[0], zs_send.at[r], zs_recv.at[0], f, there).wait_send()

        @pl.when(me < reducers)
        def _():
            remote(tile, full.at[0, 0], zg_send.at[r], zg_recv.at[0], f, there).wait_send()

    for copy in (edge, core_copy, flip_copy, to_core):
        copy.wait_send()

    @pl.when(jnp.logical_not(own_last))
    def _():
        last_copy.wait_send()


def kernel(F, C, lat_hbm, stream_hbm, q_hbm, k_hbm, v_hbm, w_hbm, wh_hbm, flip_ref, hg_ref, *scratch):
    p = Place(F, C)
    bufs = dict(zip(NAMES, scratch))
    g = bufs.__getitem__
    weights = Weights(p, *map(g, WEIGHTS))
    h, at, per = weights.own(p.f)
    early_loads = [pltpu.make_async_copy(wh_hbm, g("whv").at[h, pl.ds(at, per)], g("in_sem").at[4])]
    late = [
        pltpu.make_async_copy(stream_hbm, g("stream"), g("in_sem").at[5]),
        pltpu.make_async_copy(lat_hbm, g("lat"), g("in_sem").at[6]),
    ]
    for copy in early_loads:
        copy.start()
    entry(p, q_hbm, k_hbm, v_hbm, w_hbm, g("kbuf"), g("vbuf"), g("wbuf"), g("qbuf"), g("in_sem"))
    for copy in late:
        copy.start()
    for copy in early_loads + late:
        copy.wait()
    early, drain = attend_phase(p, weights, *map(g, ATTEND))
    head_phase(
        p, early, g("att"), g("wt"), g("stream"), g("sp"), g("mall"), g("lat"), flip_ref, hg_ref, *map(g, HEAD)
    )
    drain()
    weights.drain()


WEIGHTS = (
    "wbuf", "whv", "stream", "sp", "mp", "m_in", "m_half", "m_in2", "mall",
    "wh_send", "wh_recv", "whs_sem", "ms_sem", "mm_sem", "mg_send", "mg_recv", "mx_sem",
)
ATTEND = (
    "qbuf", "kbuf", "vbuf", "wbuf", "q2", "m_s", "l_s", "acc_s", "o_in", "st_out", "st_in", "tbuf", "att", "wt",
    "ring_send", "ring_recv", "sib_send", "sib_recv", "w_send", "w_recv", "w2_send", "w2_recv", "ws_sem", "q_sem",
    "o_send", "o_recv",
)
HEAD = (
    "attbuf", "edge_out", "edge_in", "flip_out", "flip_in", "last_out", "last_in", "part", "cbuf", "zbuf", "rbuf", "tile",
    "full", "att_send", "att_recv", "edge_sem", "flip_sem", "last_sem", "core_sem", "zs_send", "zs_recv", "zg_send",
    "zg_recv", "core2_sem",
)


def shapes(F, C, tok, width, cols, wide, chan, share):
    Z = C // 4
    per, n = Z // (F // 2), Z // 2 + 1
    tiles = share // 2 // 8
    each = -(-tiles // (2 * Z))
    reducers = tiles // each
    block = (each * 8, 2 * chan)
    dma = pltpu.SemaphoreType.DMA

    def v(*shape, dtype=F32):
        return pltpu.VMEM(shape, dtype)

    return dict(
        qbuf=v(tok, width, dtype=BF16), kbuf=v(Z, 2, tok, width, dtype=BF16), vbuf=v(Z, 2, tok, width, dtype=BF16),
        wbuf=v(Z, cols, wide, dtype=BF16), q2=v(tok, width, dtype=BF16), m_s=v(2, 2, tok, 128), l_s=v(2, 2, tok, 128),
        acc_s=v(2, 2, tok, HD), o_in=v(2, tok, HD), st_out=v(8, tok), st_in=v(8, tok), tbuf=v(128, tok),
        att=v(tok, width, dtype=BF16), wt=v(per, 2, cols, F * wide, dtype=BF16),
        ring_send=dma((4, n)), ring_recv=dma((4, n)), sib_send=dma((4, n)), sib_recv=dma((4, n)),
        w_send=dma((2, n)), w_recv=dma((2, n)), w2_send=dma((Z, 2)), w2_recv=dma((F,)), ws_sem=dma((2,)),
        q_sem=dma((2,)), o_send=dma((2,)), o_recv=dma((2,)), in_sem=dma((7,)),
        stream=v(tok, share * F, dtype=BF16), lat=v(chan, tok), whv=v(2, Z, 2, cols, 2 * chan, dtype=BF16),
        sp=v(2 * chan, tok), mp=v(2, chan, wide), m_in=v(chan, wide), m_half=v(chan, wide), m_in2=v(chan, wide),
        mall=v(2, chan, F * wide), wh_send=dma((F,)), wh_recv=dma((F,)), whs_sem=dma((2, F)), ms_sem=dma((2,)),
        mm_sem=dma((2,)), mg_send=dma((F,)), mg_recv=dma((F,)), mx_sem=dma((2,)),
        attbuf=v(tok, F * wide, dtype=BF16), edge_out=v(8, 128), edge_in=v(8, 128),
        flip_out=v(chan, tok), flip_in=v(chan, tok), last_out=v(8, 2 * chan), last_in=v(8, 2 * chan),
        part=v(2, reducers, *block), cbuf=v(reducers, *block), zbuf=v(reducers, *block), rbuf=v(2 * Z, *block),
        tile=v(*block), full=v(2, reducers, *block),
        att_send=dma((F,)), att_recv=dma((F,)), edge_sem=dma((2,)), flip_sem=dma((2,)), last_sem=dma((2,)),
        core_sem=dma((2,)), zs_send=dma((2 * Z,)), zs_recv=dma((2 * Z,)), zg_send=dma((2 * Z,)), zg_recv=dma((2 * Z,)),
        core2_sem=dma((2,)),
    )


NAMES = tuple(shapes(8, 64, 128, 256, 48, 256, 64, 384))


def shards(F, C, latents, stream, queries, key_rows, value_rows, w_mix, w_head):
    tok, chan = latents.shape
    share, chan2 = w_head.shape
    width = queries.shape[1]
    w_t = w_mix.T
    vmem = pl.BlockSpec(memory_space=pltpu.VMEM)
    flipped, grad = pl.pallas_call(
        functools.partial(kernel, F, C),
        out_shape=(
            jax.ShapeDtypeStruct((chan, tok), F32),
            jax.ShapeDtypeStruct((share, chan2), F32),
        ),
        in_specs=[pl.BlockSpec(memory_space=pl.ANY)] * 7,
        out_specs=(vmem, vmem),
        scratch_shapes=list(shapes(F, C, tok, width, *w_t.shape, chan, share).values()),
        compiler_params=pltpu.CompilerParams(
            collective_id=0, has_side_effects=True, vmem_limit_bytes=60 * 1024 * 1024
        ),
        name="coupling",
    )(latents.T, stream, queries, key_rows, value_rows, w_t, w_head.reshape(-1, 2, w_t.shape[0], chan2))
    return flipped.T, grad


def solution(mesh):
    return jax.shard_map(
        functools.partial(shards, mesh.shape["fsdp"], mesh.shape["ctx"]),
        mesh=mesh,
        in_specs=(
            P("ctx", None),
            P("ctx", None),
            P("ctx", "fsdp"),
            P("ctx", "fsdp"),
            P("ctx", "fsdp"),
            P("fsdp", "ctx"),
            P("fsdp", None),
        ),
        out_specs=(P("ctx", None), P("fsdp", None)),
        check_vma=False,
    )
```

time: 126 us -> 113 us (0.90)
  Pallas kernels: 117 us -> 109 us
  local copies, waits for them, and re-layouts: 7.5 us -> 2.99 us
    pallas_call x2 -> x1, Pallas kernels: 117 us -> 109 us  [shards(): pl.pallas_call(functools.partial(kernel, F, C), out_shape=(jax.ShapeDtype...]
    unnamed x14 -> x2, local copies, waits for them, and re-layouts: 6.8 us -> 2.99 us
where the time goes in v2:
time: 113 us
  Pallas kernels  109 us (96%)
  local copies, waits for them, and re-layouts  2.99 us (3%)
    pallas_call x1, Pallas kernels, shards(): pl.pallas_call(functools.partial(kernel, F, C), out_shape=(jax.ShapeDtype...  109 us
    unnamed x2, local copies, waits for them, and re-layouts  2.99 us

profile of v2, /device:TPU:1, one launch (start us, length us, event | category | flops | bytes accessed | tf_op | source)
XLA Modules:
  0.0 113.1 jit_solution(17216441021204211348)
XLA Ops:
  0.6 109.5 %coupling.1 = (f32[64,128]{1,0:T(8,128)}, f32[384,128]{1,0:T(8,128)}) custom-call(f32[64,128]{1,0:T(8,128)} %bitcast.5, bf16[128,3072]{1,0:T(8,128)(2,1)} %stream_hbm.1, bf16[128,256]{1,0:T(8,128)(2,1)} %q_hbm.1, bf16[128,256]{1,0:T(8,128)(2,1)} %k_hbm.1, bf16[128,256]{1,0:T(8,128)(2,1)} %v_hbm.1, bf16[48,256]{1,0:T(8,128)(2,1)} %bitcast.7, ...), custom_call_target="tpu_custom_call" | custom-call | tf_op jit(solution)/shard_map/coupling/pallas_call | solution.py:771
  110.1 1.4 %copy.11 = f32[128,64]{0,1:T(8,128)} copy(f32[128,64]{0,1:T(8,128)} %bitcast.6) | data formatting | bytes 65536
  111.5 1.6 %copy.12 = f32[384,128]{1,0:T(8,128)} copy(f32[384,128]{1,0:T(8,128)} %get-tuple-element.9) | data formatting | bytes 393216

commit v3 on v2

--- a/solution.py
+++ b/solution.py
@@ -143,7 +143,6 @@
         out = jnp.dot(rows.astype(F32).T.astype(BF16), pieces, preferred_element_type=F32)
         self.mp[...] = out.reshape(self.mp.shape)
         self.to_sib.start()
-        self.sp[...] = jnp.dot(self.stream[...], self.whv[...].reshape(-1, 128), preferred_element_type=F32).T
 
     def halves(self):
         self.to_sib.wait_recv()
@@ -174,6 +173,7 @@
 
     def finish(self):
         p = self.p
+        self.sp[...] = jnp.dot(self.stream[...], self.whv[...].reshape(-1, 128), preferred_element_type=F32).T
 
         @pl.loop(1, p.F)
         def _(r):
@@ -253,27 +253,34 @@
 
     weights.start()
 
-    def fold(who, o, masked=False):
+    def fold(who, blocks, masked=False):
+        q = q_ref if who == 0 else q2
+        heads = [slice(h * HD, (h + 1) * HD) for h in range(2)]
+
+        def rows(ref, o, h):
+            return ref[o, :, :, heads[h]].reshape(2 * tok, HD)
+
+        scores = [[dot_nt(q[:, heads[h]], rows(kbuf, o, h)) for o in blocks] for h in range(2)]
+        if masked:
+            at = lax.broadcasted_iota(jnp.int32, (tok, 2 * tok), 1)
+            seen = at <= k * tok + lax.broadcasted_iota(jnp.int32, (tok, 2 * tok), 0)
+            scores = [[jnp.where(seen, x, -1e30) for x in per_head] for per_head in scores]
+        parts, m_old, m_new = [], [], []
         for h in range(2):
-            cols = slice(h * HD, (h + 1) * HD)
-            q = (q_ref if who == 0 else q2)[:, cols]
-            kk = kbuf[o, :, :, cols].reshape(2 * tok, HD)
-            vv = vbuf[o, :, :, cols].reshape(2 * tok, HD)
-            s = dot_nt(q, kk)
-            if masked:
-                row = k * tok + lax.broadcasted_iota(jnp.int32, s.shape, 0)
-                s = jnp.where(lax.broadcasted_iota(jnp.int32, s.shape, 1) <= row, s, -1e30)
-            s0, s1 = s[:, :tok], s[:, tok:]
-            m_old = m_s[who, h]
-            top = jnp.max(jnp.maximum(s0, s1), axis=1, keepdims=True)
-            m_new = jnp.maximum(m_old, top)
-            keep = jnp.exp2((m_old - m_new) * SCALE)
-            p0 = jnp.exp2((s0 - m_new) * SCALE)
-            p1 = jnp.exp2((s1 - m_new) * SCALE)
-            m_s[who, h] = m_new
-            l_s[who, h] = l_s[who, h] * keep + (p0 + p1)
-            both = jnp.concatenate([p0.astype(BF16), p1.astype(BF16)], axis=1)
-            acc_s[who, h] = acc_s[who, h] * keep + jnp.dot(both, vv, preferred_element_type=F32)
+            parts.append([x[:, i * tok : (i + 1) * tok] for x in scores[h] for i in range(2)])
+            top = jnp.max(functools.reduce(jnp.maximum, parts[h]), axis=1, keepdims=True)
+            m_old.append(m_s[who, h])
+            m_new.append(jnp.maximum(m_old[h], top))
+        for h in range(2):
+            keep = jnp.exp2((m_old[h] - m_new[h]) * SCALE)
+            e = [jnp.exp2((x - m_new[h]) * SCALE) for x in parts[h]]
+            m_s[who, h] = m_new[h]
+            l_s[who, h] = l_s[who, h] * keep + functools.reduce(jnp.add, e)
+            acc = acc_s[who, h] * keep
+            for i, o in enumerate(blocks):
+                both = jnp.concatenate([e[2 * i].astype(BF16), e[2 * i + 1].astype(BF16)], axis=1)
+                acc = acc + jnp.dot(both, rows(vbuf, o, h), preferred_element_type=F32)
+            acc_s[who, h] = acc
 
     def arrive(kind, s):
         o = origin(kind, s)
@@ -338,25 +345,31 @@
         @pl.when(half == 0)
         def _():
             to_mate.wait_recv()
-            fold(1, z)
-
-        fold(0, z, masked=True)
+            fold(1, (z,))
+
+        fold(0, (z,), masked=True)
 
     def fold_step(s):
-        for base in (0, 2):
-            o = origin(base, s)
-            beside(base, s, 1 - k).wait_recv()
-            beside(base + 1, s, 1 - k).wait_recv()
-
-            @pl.when(half == 0)
-            def _():
-                fold(1, o)
-
-            seen = z >= s if base == 0 else z + s >= Z
-
-            @pl.when(seen)
-            def _():
-                fold(0, o)
+        low, high = origin(0, s), origin(2, s)
+        for kind in range(4):
+            beside(kind, s, 1 - k).wait_recv()
+        from_low, from_high = z >= s, z + s >= Z
+
+        @pl.when(half == 0)
+        def _():
+            fold(1, (low, high))
+
+        @pl.when(jnp.logical_and(from_low, from_high))
+        def _():
+            fold(0, (low, high))
+
+        @pl.when(jnp.logical_and(from_low, jnp.logical_not(from_high)))
+        def _():
+            fold(0, (low,))
+
+        @pl.when(jnp.logical_and(from_high, jnp.logical_not(from_low)))
+        def _():
+            fold(0, (high,))
 
     to_plane(z)
 
@@ -391,26 +404,25 @@
         def _():
             arrive(3, s)
 
-        @pl.when(s <= steps // 2)
-        def _():
-            w_arrive(s)
+        @pl.when(jnp.logical_and(s > 1, s <= steps // 2 + 1))
+        def _():
+            w_arrive(s - 1)
 
         @pl.when(s == 3)
         def _():
             weights.share()
 
-        @pl.when(s == steps // 2)
+        @pl.when(s == steps // 2 + 1)
         def _():
             weights.partial()
 
-        @pl.when(s == steps // 2 + 1)
+        @pl.when(s == steps // 2 + 2)
         def _():
             weights.halves()
 
-        @pl.when(s == steps - 1)
+        @pl.when(s == steps)
         def _():
             weights.gather()
-            collect()
 
         @pl.when(s == 1)
         def _():
@@ -431,7 +443,7 @@
 
     @pl.when(half == 0)
     def _():
-        fold(1, far)
+        fold(1, (far,))
         back[0].start()
         stats = jnp.zeros((tok, 128), F32)
         for h in range(2):
@@ -442,7 +454,9 @@
 
     @pl.when(z >= steps)
     def _():
-        fold(0, far)
+        fold(0, (far,))
+
+    collect()
 
     def store(h, acc, total):
         att_ref[:, h * HD : (h + 1) * HD] = (acc / total).astype(BF16)
@@ -611,16 +625,6 @@
         def _():
             remote(zbuf.at[to], rbuf.at[me], zs_send.at[r], zs_recv.at[me], f, there).start()
 
-    flip_copy.start()
-
-    @pl.when(own_last)
-    def _():
-        last_in[...] = last_out[...]
-
-    @pl.when(jnp.logical_not(own_last))
-    def _():
-        last_copy.start()
-
     @pl.when(me < reducers)
     def _():
         rbuf[me] = zbuf[me]
@@ -637,6 +641,16 @@
             remote(tile, full.at[k, me], zg_send.at[r], zg_recv.at[me], f, rank(r)[1]).start()
 
         full[k, me] = tile[...]
+
+    flip_copy.start()
+
+    @pl.when(own_last)
+    def _():
+        last_in[...] = last_out[...]
+
+    @pl.when(jnp.logical_not(own_last))
+    def _():
+        last_copy.start()
 
     flip_copy.wait_recv()
 

time: 113 us -> 109 us (0.965); the launches traced: 113 us -> 108 us
  Pallas kernels: 109 us -> 104 us
    pallas_call x1, Pallas kernels: 109 us -> 104 us  [shards(): pl.pallas_call(functools.partial(kernel, F, C), out_shape=(jax.ShapeDtype...]
where the time goes in v3:
time: 109 us; the launch traced here: 108 us
  Pallas kernels  104 us (95%)
  local copies, waits for them, and re-layouts  2.99 us (3%)
    pallas_call x1, Pallas kernels, shards(): pl.pallas_call(functools.partial(kernel, F, C), out_shape=(jax.ShapeDtype...  104 us
    unnamed x2, local copies, waits for them, and re-layouts  2.99 us

profile of v3, /device:TPU:1, one launch (start us, length us, event | category | flops | bytes accessed | tf_op | source)
XLA Modules:
  0.0 107.9 jit_solution(285769328543927846)
XLA Ops:
  0.6 104.3 %coupling.1 = (f32[64,128]{1,0:T(8,128)}, f32[384,128]{1,0:T(8,128)}) custom-call(f32[64,128]{1,0:T(8,128)} %bitcast.5, bf16[128,3072]{1,0:T(8,128)(2,1)} %stream_hbm.1, bf16[128,256]{1,0:T(8,128)(2,1)} %q_hbm.1, bf16[128,256]{1,0:T(8,128)(2,1)} %k_hbm.1, bf16[128,256]{1,0:T(8,128)(2,1)} %v_hbm.1, bf16[48,256]{1,0:T(8,128)(2,1)} %bitcast.7, ...), custom_call_target="tpu_custom_call" | custom-call | tf_op jit(solution)/shard_map/coupling/pallas_call | solution.py:785
  104.9 1.4 %copy.11 = f32[128,64]{0,1:T(8,128)} copy(f32[128,64]{0,1:T(8,128)} %bitcast.6) | data formatting | bytes 65536
  106.3 1.6 %copy.12 = f32[384,128]{1,0:T(8,128)} copy(f32[384,128]{1,0:T(8,128)} %get-tuple-element.9) | data formatting | bytes 393216

commit v4 on v3

--- a/solution.py
+++ b/solution.py
@@ -533,14 +533,14 @@
 
 def head_phase(
     p, early, att_ref, wt_ref, stream, sp, mall, lat_ref, flip_ref, hg_ref,
-    attbuf, edge_out, edge_in, flip_out, flip_in, last_out, last_in, part, cbuf, zbuf, rbuf, tile, full,
-    att_send, att_recv, edge_sem, flip_sem, last_sem, core_sem, zs_send, zs_recv, zg_send, zg_recv, core2_sem,
+    attbuf, edge_out, edge_in, flip_out, flip_in, last_out, last_in, part, cbuf, zbuf, nbuf, hbuf, hbuf_in, qbuf, full,
+    att_send, att_recv, edge_sem, flip_sem, last_sem, core_sem, half_sem, zs_send, zs_recv, zq_send, zq_recv,
+    zg_send, zg_recv, core2_sem,
 ):
     F, C = p.F, p.C
     f, c, z, k, half, Z = p.f, p.c, p.z, p.k, p.half, p.Z
     tok, wide = att_ref.shape
     chan = lat_ref.shape[0]
-    reducers = zbuf.shape[0]
     mirror, mirror2 = C - 1 - c, lax.rem(2 * C - 2 - c, C)
     own_last = mirror2 == c
     lane = lax.broadcasted_iota(jnp.int32, (chan, tok), 1)
@@ -610,38 +610,32 @@
 
     core_copy.wait_recv()
     zbuf[...] = part[k] + cbuf[...]
-    ranks = 2 * Z
-    me = half * Z + z
-
-    def rank(r):
-        i = lax.rem(me + r, ranks)
-        return i, p.at(i // Z, lax.rem(i, Z), k)
-
-    @pl.loop(1, ranks)
-    def _(r):
-        to, there = rank(r)
-
-        @pl.when(to < reducers)
-        def _():
-            remote(zbuf.at[to], rbuf.at[me], zs_send.at[r], zs_recv.at[me], f, there).start()
-
-    @pl.when(me < reducers)
-    def _():
-        rbuf[me] = zbuf[me]
-
-        @pl.loop(1, ranks)
-        def _(r):
-            i, there = rank(r)
-            remote(zbuf.at[0], rbuf.at[i], zs_send.at[r], zs_recv.at[i], f, there).wait_recv()
-
-        tile[...] = jnp.sum(rbuf[...], axis=0)
-
-        @pl.loop(1, ranks)
-        def _(r):
-            remote(tile, full.at[k, me], zg_send.at[r], zg_recv.at[me], f, rank(r)[1]).start()
-
-        full[k, me] = tile[...]
-
+    g, q = lax.rem(z, 4), z // 4
+    quads = Z // 4
+
+    def near(r):
+        i = lax.rem(g + r, 4)
+        return i, p.at(half, q * 4 + i, k)
+
+    def far(r):
+        i = lax.rem(q + r, quads)
+        return i, p.at(half, i * 4 + g, k)
+
+    for r in range(1, 4):
+        i, there = near(r)
+        remote(zbuf.at[i], nbuf.at[g], zs_send.at[r], zs_recv.at[g], f, there).start()
+    nbuf[g] = zbuf[g]
+    for r in range(1, 4):
+        i, there = near(r)
+        remote(zbuf.at[i], nbuf.at[i], zs_send.at[r], zs_recv.at[i], f, there).wait_recv()
+    hbuf[...] = nbuf[0] + nbuf[1] + nbuf[2] + nbuf[3]
+    half_copy = remote(hbuf, hbuf_in, half_sem.at[0], half_sem.at[1], f, p.mate)
+    half_copy.start()
+    half_copy.wait_recv()
+    qbuf[q] = hbuf[...] + hbuf_in[...]
+    for r in range(1, quads):
+        i, there = far(r)
+        remote(qbuf.at[q], qbuf.at[q], zq_send.at[r], zq_recv.at[q], f, there).start()
     flip_copy.start()
 
     @pl.when(own_last)
@@ -652,6 +646,14 @@
     def _():
         last_copy.start()
 
+    for r in range(1, quads):
+        i, there = far(r)
+        remote(qbuf.at[i], qbuf.at[i], zq_send.at[r], zq_recv.at[i], f, there).wait_recv()
+    full[k, g] = functools.reduce(jnp.add, [qbuf[i] for i in range(quads)])
+    for r in range(1, 4):
+        i, there = near(r)
+        remote(full.at[k, g], full.at[k, g], zg_send.at[r], zg_recv.at[g], f, there).start()
+
     flip_copy.wait_recv()
 
     @pl.when(jnp.logical_not(own_last))
@@ -660,14 +662,9 @@
 
     flip_ref[...] = jnp.where(lane == tok - 1, as_column(last_in[7:8])[:chan], flip_in[...])
 
-    @pl.loop(1, ranks)
-    def _(r):
-        i, there = rank(r)
-
-        @pl.when(i < reducers)
-        def _():
-            remote(tile, full.at[k, i], zg_send.at[r], zg_recv.at[i], f, there).wait_recv()
-
+    for r in range(1, 4):
+        i, there = near(r)
+        remote(full.at[k, i], full.at[k, i], zg_send.at[r], zg_recv.at[i], f, there).wait_recv()
     to_core = remote(full.at[k], full.at[k], core2_sem.at[0], core2_sem.at[1], f, p.sib)
     to_core.start()
     remote(full.at[1 - k], full.at[1 - k], core2_sem.at[0], core2_sem.at[1], f, p.sib).wait_recv()
@@ -677,19 +674,15 @@
     def _(r):
         att_copy(r).wait_send()
 
-    @pl.loop(1, ranks)
-    def _(r):
-        i, there = rank(r)
-
-        @pl.when(i < reducers)
-        def _():
-            remote(zbuf.at[0], rbuf.at[0], zs_send.at[r], zs_recv.at[0], f, there).wait_send()
-
-        @pl.when(me < reducers)
-        def _():
-            remote(tile, full.at[0, 0], zg_send.at[r], zg_recv.at[0], f, there).wait_send()
-
-    for copy in (edge, core_copy, flip_copy, to_core):
+    for r in range(1, 4):
+        i, there = near(r)
+        remote(zbuf.at[i], nbuf.at[0], zs_send.at[r], zs_recv.at[0], f, there).wait_send()
+        remote(full.at[k, g], full.at[k, g], zg_send.at[r], zg_recv.at[0], f, there).wait_send()
+    for r in range(1, quads):
+        i, there = far(r)
+        remote(qbuf.at[q], qbuf.at[q], zq_send.at[r], zq_recv.at[0], f, there).wait_send()
+
+    for copy in (edge, core_copy, half_copy, flip_copy, to_core):
         copy.wait_send()
 
     @pl.when(jnp.logical_not(own_last))
@@ -733,19 +726,16 @@
     "o_send", "o_recv",
 )
 HEAD = (
-    "attbuf", "edge_out", "edge_in", "flip_out", "flip_in", "last_out", "last_in", "part", "cbuf", "zbuf", "rbuf", "tile",
-    "full", "att_send", "att_recv", "edge_sem", "flip_sem", "last_sem", "core_sem", "zs_send", "zs_recv", "zg_send",
-    "zg_recv", "core2_sem",
+    "attbuf", "edge_out", "edge_in", "flip_out", "flip_in", "last_out", "last_in", "part", "cbuf", "zbuf", "nbuf", "hbuf",
+    "hbuf_in", "quart", "full", "att_send", "att_recv", "edge_sem", "flip_sem", "last_sem", "core_sem", "half_sem",
+    "zs_send", "zs_recv", "zq_send", "zq_recv", "zg_send", "zg_recv", "core2_sem",
 )
 
 
 def shapes(F, C, tok, width, cols, wide, chan, share):
     Z = C // 4
     per, n = Z // (F // 2), Z // 2 + 1
-    tiles = share // 2 // 8
-    each = -(-tiles // (2 * Z))
-    reducers = tiles // each
-    block = (each * 8, 2 * chan)
+    block = (share // 8, 2 * chan)
     dma = pltpu.SemaphoreType.DMA
 
     def v(*shape, dtype=F32):
@@ -765,11 +755,11 @@
         mm_sem=dma((2,)), mg_send=dma((F,)), mg_recv=dma((F,)), mx_sem=dma((2,)),
         attbuf=v(tok, F * wide, dtype=BF16), edge_out=v(8, 128), edge_in=v(8, 128),
         flip_out=v(chan, tok), flip_in=v(chan, tok), last_out=v(8, 2 * chan), last_in=v(8, 2 * chan),
-        part=v(2, reducers, *block), cbuf=v(reducers, *block), zbuf=v(reducers, *block), rbuf=v(2 * Z, *block),
-        tile=v(*block), full=v(2, reducers, *block),
+        part=v(2, 4, *block), cbuf=v(4, *block), zbuf=v(4, *block), nbuf=v(4, *block), hbuf=v(*block), hbuf_in=v(*block),
+        quart=v(Z // 4, *block), full=v(2, 4, *block),
         att_send=dma((F,)), att_recv=dma((F,)), edge_sem=dma((2,)), flip_sem=dma((2,)), last_sem=dma((2,)),
-        core_sem=dma((2,)), zs_send=dma((2 * Z,)), zs_recv=dma((2 * Z,)), zg_send=dma((2 * Z,)), zg_recv=dma((2 * Z,)),
-        core2_sem=dma((2,)),
+        core_sem=dma((2,)), half_sem=dma((2,)), zs_send=dma((4,)), zs_recv=dma((4,)), zq_send=dma((Z // 4,)),
+        zq_recv=dma((Z // 4,)), zg_send=dma((4,)), zg_recv=dma((4,)), core2_sem=dma((2,)),
     )
 
 

time: 109 us -> 106 us (0.972); the launches traced: 108 us -> 106 us
  Pallas kernels: 104 us -> 102 us
    pallas_call x1, Pallas kernels: 104 us -> 102 us  [shards(): pl.pallas_call(functools.partial(kernel, F, C), out_shape=(jax.ShapeDtype...]
where the time goes in v4:
time: 106 us
  Pallas kernels  102 us (96%)
  local copies, waits for them, and re-layouts  2.99 us (3%)
    pallas_call x1, Pallas kernels, shards(): pl.pallas_call(functools.partial(kernel, F, C), out_shape=(jax.ShapeDtype...  102 us
    unnamed x2, local copies, waits for them, and re-layouts  2.99 us

profile of v4, /device:TPU:1, one launch (start us, length us, event | category | flops | bytes accessed | tf_op | source)
XLA Modules:
  0.0 106.0 jit_solution(5769640574490582528)
XLA Ops:
  0.6 102.4 %coupling.1 = (f32[64,128]{1,0:T(8,128)}, f32[384,128]{1,0:T(8,128)}) custom-call(f32[64,128]{1,0:T(8,128)} %bitcast.5, bf16[128,3072]{1,0:T(8,128)(2,1)} %stream_hbm.1, bf16[128,256]{1,0:T(8,128)(2,1)} %q_hbm.1, bf16[128,256]{1,0:T(8,128)(2,1)} %k_hbm.1, bf16[128,256]{1,0:T(8,128)(2,1)} %v_hbm.1, bf16[48,256]{1,0:T(8,128)(2,1)} %bitcast.7, ...), custom_call_target="tpu_custom_call" | custom-call | tf_op jit(solution)/shard_map/coupling/pallas_call | solution.py:775
  103.1 1.4 %copy.11 = f32[128,64]{0,1:T(8,128)} copy(f32[128,64]{0,1:T(8,128)} %bitcast.6) | data formatting | bytes 65536
  104.4 1.6 %copy.12 = f32[384,128]{1,0:T(8,128)} copy(f32[384,128]{1,0:T(8,128)} %get-tuple-element.9) | data formatting | bytes 393216

commit v5 on v4

--- a/solution.py
+++ b/solution.py
@@ -86,12 +86,13 @@
 
 class Weights:
     def __init__(
-        self, p, wbuf, whv, stream, sp, mp, m_in, m_half, m_in2, mall,
-        wh_send, wh_recv, whs_sem, ms_sem, mm_sem, mg_send, mg_recv, mx_sem,
+        self, p, wbuf, whv, stream, sp, mp, m_in, m_half, m_in2, mall, m3,
+        wh_send, wh_recv, whs_sem, ms_sem, mm_sem, mx_sem,
     ):
         self.p, self.wbuf, self.whv, self.stream, self.sp = p, wbuf, whv, stream, sp
         self.mp, self.m_in, self.m_half, self.m_in2, self.mall = mp, m_in, m_half, m_in2, mall
-        self.wh_sems, self.mg_sems = (wh_send, wh_recv), (mg_send, mg_recv)
+        self.m3 = m3
+        self.wh_sems = (wh_send, wh_recv)
         f, k = p.f, p.k
         self.whs_sem, self.mx_sem = whs_sem, mx_sem
         self.to_sib = remote(mp.at[1 - k], m_in, ms_sem.at[0], ms_sem.at[1], f, p.sib)
@@ -149,38 +150,21 @@
         self.m_half[...] = self.mp[self.p.k] + self.m_in[...]
         self.to_mate.start()
 
-    def lanes(self, fs):
-        width = self.mp.shape[2]
-        return pl.ds(pl.multiple_of(fs * width, width), width)
-
-    def all_copy(self, r, fs):
-        p = self.p
-        send, recv = self.mg_sems
-        dst = self.mall.at[p.k, :, self.lanes(fs)]
-        return remote(dst, dst, send.at[r], recv.at[fs], lax.rem(p.f + r, p.F), p.c)
-
-    def gather(self):
-        p = self.p
+    def whole(self):
         self.to_mate.wait_recv()
-        self.mall[p.k, :, self.lanes(p.f)] = self.m_half[...] + self.m_in2[...]
-
-        @pl.loop(1, p.F)
-        def _(r):
-            self.all_copy(r, p.f).start()
+        self.mall[self.p.k] = self.m_half[...] + self.m_in2[...]
+        self.across(self.p.k).start()
 
     def across(self, core):
         return remote(self.mall.at[core], self.mall.at[core], self.mx_sem.at[0], self.mx_sem.at[1], self.p.f, self.p.sib)
 
-    def finish(self):
-        p = self.p
+    def settle(self):
+        self.across(1 - self.p.k).wait_recv()
+        for i, part in enumerate(split3(self.mall[...].reshape(self.m3.shape[1:]))):
+            self.m3[i] = part
+
+    def stream_part(self):
         self.sp[...] = jnp.dot(self.stream[...], self.whv[...].reshape(-1, 128), preferred_element_type=F32).T
-
-        @pl.loop(1, p.F)
-        def _(r):
-            self.all_copy(r, lax.rem(p.f + r, p.F)).wait_recv()
-
-        self.across(p.k).start()
-        self.across(1 - p.k).wait_recv()
 
     def drain(self):
         p = self.p
@@ -189,7 +173,6 @@
         def _(r):
             self.head_copy(r, p.f).wait_send()
             self.beside(p.k, lax.rem(p.f + r, p.F)).wait_send()
-            self.all_copy(r, p.f).wait_send()
 
         self.to_sib.wait_send()
         self.to_mate.wait_send()
@@ -422,7 +405,7 @@
 
         @pl.when(s == steps)
         def _():
-            weights.gather()
+            weights.whole()
 
         @pl.when(s == 1)
         def _():
@@ -456,6 +439,7 @@
     def _():
         fold(0, (far,))
 
+    weights.settle()
     collect()
 
     def store(h, acc, total):
@@ -482,7 +466,7 @@
             store(h, acc_s[0, h] * e_a + o_in[h] * e_b, l_a * e_a + l_b * e_b)
 
     def early():
-        weights.finish()
+        weights.stream_part()
         remote(wt_ref.at[:, 1 - k], wt_ref.at[:, 1 - k], ws_sem.at[0], ws_sem.at[1], f, p.sib).wait_recv()
 
     def drain():
@@ -532,9 +516,9 @@
 
 
 def head_phase(
-    p, early, att_ref, wt_ref, stream, sp, mall, lat_ref, flip_ref, hg_ref,
+    p, early, att_ref, wt_ref, stream, sp, m3, lat_ref, flip_ref, hg_ref, pp, rs, pall, psum,
     attbuf, edge_out, edge_in, flip_out, flip_in, last_out, last_in, part, cbuf, zbuf, nbuf, hbuf, hbuf_in, qbuf, full,
-    att_send, att_recv, edge_sem, flip_sem, last_sem, core_sem, half_sem, zs_send, zs_recv, zq_send, zq_recv,
+    rs_send, rs_recv, ag_send, ag_recv, att_send, att_recv, edge_sem, flip_sem, last_sem, core_sem, half_sem, zs_send, zs_recv, zq_send, zq_recv,
     zg_send, zg_recv, core2_sem,
 ):
     F, C = p.F, p.C
@@ -549,6 +533,14 @@
         return jnp.broadcast_to(row, (tok, 128)).T
 
     mine = pl.ds(pl.multiple_of(f * wide, wide), wide)
+    own = att_ref[...]
+    pp[...] = (dot_nt(m3[2], own) + dot_nt(m3[1], own) + dot_nt(m3[0], own)).reshape(pp.shape)
+
+    @pl.loop(1, F)
+    def _(r):
+        to = lax.rem(f + r, F)
+        remote(pp.at[to], rs.at[f], rs_send.at[r], rs_recv.at[f], to, c).start()
+
     attbuf[:, mine] = att_ref[...]
 
     def att_copy(r):
@@ -565,9 +557,22 @@
     edge = remote(edge_out, edge_in, edge_sem.at[0], edge_sem.at[1], f, p.prev)
     edge.start()
     share = hg_ref.shape[0]
+    rs[f] = pp[f]
+
+    @pl.loop(1, F)
+    def _(r):
+        fs = lax.rem(f + r, F)
+        remote(pp.at[fs], rs.at[fs], rs_send.at[r], rs_recv.at[fs], fs, c).wait_recv()
+
+    psum[...] = jnp.sum(rs[...], axis=0)
+
+    @pl.loop(1, F)
+    def _(r):
+        remote(psum, pall.at[f], ag_send.at[r], ag_recv.at[f], lax.rem(f + r, F), c).start()
+
+    pall[f] = psum[...]
     stream_t = stream[:, pl.ds(pl.multiple_of(f * share, 128), share)].astype(F32).T
     early()
-    m_all = split3(mall[...].reshape(2 * chan, F * wide))
     edge.wait_recv()
     lat_next = jnp.where(lane == tok - 1, as_column(edge_in[0:1])[:chan], pltpu.roll(lat_t, tok - 1, 1))
 
@@ -578,9 +583,15 @@
         remote(att_ref, attbuf.at[:, there], att_send.at[r], att_recv.at[fs], fs, c).wait_recv()
 
     heads = attbuf[...]
-    pred = sp[...] + (dot_nt(m_all[2], heads) + dot_nt(m_all[1], heads) + dot_nt(m_all[0], heads))
     resid = stream_t + dot_nt(wt_ref[...].reshape(share, F * wide), heads)
     r_hi, r_mid, r_lo = split3(resid)
+
+    @pl.loop(1, F)
+    def _(r):
+        fs = lax.rem(f + r, F)
+        remote(psum, pall.at[fs], ag_send.at[r], ag_recv.at[fs], fs, c).wait_recv()
+
+    pred = sp[...] + pall[...].reshape(2 * chan, tok)
     final = jnp.logical_and(c == C - 1, lane == tok - 1)
     shift = jnp.where(final, 0.0, pred[:chan])
     log_scale = jnp.where(final, 0.0, pred[chan:])
@@ -673,6 +684,8 @@
     @pl.loop(1, F)
     def _(r):
         att_copy(r).wait_send()
+        remote(pp.at[0], rs.at[0], rs_send.at[r], rs_recv.at[0], lax.rem(f + r, F), c).wait_send()
+        remote(psum, pall.at[0], ag_send.at[r], ag_recv.at[0], lax.rem(f + r, F), c).wait_send()
 
     for r in range(1, 4):
         i, there = near(r)
@@ -710,15 +723,15 @@
         copy.wait()
     early, drain = attend_phase(p, weights, *map(g, ATTEND))
     head_phase(
-        p, early, g("att"), g("wt"), g("stream"), g("sp"), g("mall"), g("lat"), flip_ref, hg_ref, *map(g, HEAD)
+        p, early, g("att"), g("wt"), g("stream"), g("sp"), g("m3"), g("lat"), flip_ref, hg_ref, *map(g, HEAD)
     )
     drain()
     weights.drain()
 
 
 WEIGHTS = (
-    "wbuf", "whv", "stream", "sp", "mp", "m_in", "m_half", "m_in2", "mall",
-    "wh_send", "wh_recv", "whs_sem", "ms_sem", "mm_sem", "mg_send", "mg_recv", "mx_sem",
+    "wbuf", "whv", "stream", "sp", "mp", "m_in", "m_half", "m_in2", "mall", "m3",
+    "wh_send", "wh_recv", "whs_sem", "ms_sem", "mm_sem", "mx_sem",
 )
 ATTEND = (
     "qbuf", "kbuf", "vbuf", "wbuf", "q2", "m_s", "l_s", "acc_s", "o_in", "st_out", "st_in", "tbuf", "att", "wt",
@@ -726,8 +739,8 @@
     "o_send", "o_recv",
 )
 HEAD = (
-    "attbuf", "edge_out", "edge_in", "flip_out", "flip_in", "last_out", "last_in", "part", "cbuf", "zbuf", "nbuf", "hbuf",
-    "hbuf_in", "quart", "full", "att_send", "att_recv", "edge_sem", "flip_sem", "last_sem", "core_sem", "half_sem",
+    "pp", "rs", "pall", "psum", "attbuf", "edge_out", "edge_in", "flip_out", "flip_in", "last_out", "last_in", "part", "cbuf", "zbuf", "nbuf", "hbuf",
+    "hbuf_in", "quart", "full", "rs_send", "rs_recv", "ag_send", "ag_recv", "att_send", "att_recv", "edge_sem", "flip_sem", "last_sem", "core_sem", "half_sem",
     "zs_send", "zs_recv", "zq_send", "zq_recv", "zg_send", "zg_recv", "core2_sem",
 )
 
@@ -751,8 +764,10 @@
         q_sem=dma((2,)), o_send=dma((2,)), o_recv=dma((2,)), in_sem=dma((7,)),
         stream=v(tok, share * F, dtype=BF16), lat=v(chan, tok), whv=v(2, Z, 2, cols, 2 * chan, dtype=BF16),
         sp=v(2 * chan, tok), mp=v(2, chan, wide), m_in=v(chan, wide), m_half=v(chan, wide), m_in2=v(chan, wide),
-        mall=v(2, chan, F * wide), wh_send=dma((F,)), wh_recv=dma((F,)), whs_sem=dma((2, F)), ms_sem=dma((2,)),
-        mm_sem=dma((2,)), mg_send=dma((F,)), mg_recv=dma((F,)), mx_sem=dma((2,)),
+        mall=v(2, chan, wide), m3=v(3, 2 * chan, wide, dtype=BF16), pp=v(F, 2 * chan // F, tok),
+        rs=v(F, 2 * chan // F, tok), pall=v(F, 2 * chan // F, tok), psum=v(2 * chan // F, tok),
+        rs_send=dma((F,)), rs_recv=dma((F,)), ag_send=dma((F,)), ag_recv=dma((F,)), wh_send=dma((F,)), wh_recv=dma((F,)), whs_sem=dma((2, F)), ms_sem=dma((2,)),
+        mm_sem=dma((2,)), mx_sem=dma((2,)),
         attbuf=v(tok, F * wide, dtype=BF16), edge_out=v(8, 128), edge_in=v(8, 128),
         flip_out=v(chan, tok), flip_in=v(chan, tok), last_out=v(8, 2 * chan), last_in=v(8, 2 * chan),
         part=v(2, 4, *block), cbuf=v(4, *block), zbuf=v(4, *block), nbuf=v(4, *block), hbuf=v(*block), hbuf_in=v(*block),

time: 106 us -> 105 us (level)
    pallas_call x1, Pallas kernels: 102 us -> 101 us  [shards(): pl.pallas_call(functools.partial(kernel, F, C), out_shape=(jax.ShapeDtype...]
where the time goes in v5:
time: 105 us; the launch traced here: 104 us
  Pallas kernels  101 us (96%)
  local copies, waits for them, and re-layouts  2.99 us (3%)
    pallas_call x1, Pallas kernels, shards(): pl.pallas_call(functools.partial(kernel, F, C), out_shape=(jax.ShapeDtype...  101 us
    unnamed x2, local copies, waits for them, and re-layouts  2.99 us

profile of v5, /device:TPU:1, one launch (start us, length us, event | category | flops | bytes accessed | tf_op | source)
XLA Modules:
  0.0 104.3 jit_solution(5723136988686519701)
XLA Ops:
  0.6 100.6 %coupling.1 = (f32[64,128]{1,0:T(8,128)}, f32[384,128]{1,0:T(8,128)}) custom-call(f32[64,128]{1,0:T(8,128)} %bitcast.5, bf16[128,3072]{1,0:T(8,128)(2,1)} %stream_hbm.1, bf16[128,256]{1,0:T(8,128)(2,1)} %q_hbm.1, bf16[128,256]{1,0:T(8,128)(2,1)} %k_hbm.1, bf16[128,256]{1,0:T(8,128)(2,1)} %v_hbm.1, bf16[48,256]{1,0:T(8,128)(2,1)} %bitcast.7, ...), custom_call_target="tpu_custom_call" | custom-call | tf_op jit(solution)/shard_map/coupling/pallas_call | solution.py:790
  101.3 1.4 %copy.11 = f32[128,64]{0,1:T(8,128)} copy(f32[128,64]{0,1:T(8,128)} %bitcast.6) | data formatting | bytes 65536
  102.6 1.6 %copy.12 = f32[384,128]{1,0:T(8,128)} copy(f32[384,128]{1,0:T(8,128)} %get-tuple-element.9) | data formatting | bytes 393216

commit v6 on v5

--- a/solution.py
+++ b/solution.py
@@ -516,7 +516,7 @@
 
 
 def head_phase(
-    p, early, att_ref, wt_ref, stream, sp, m3, lat_ref, flip_ref, hg_ref, pp, rs, pall, psum,
+    p, early, drain, att_ref, wt_ref, stream, sp, m3, lat_ref, flip_ref, hg_ref, pp, rs, pall, psum,
     attbuf, edge_out, edge_in, flip_out, flip_in, last_out, last_in, part, cbuf, zbuf, nbuf, hbuf, hbuf_in, qbuf, full,
     rs_send, rs_recv, ag_send, ag_recv, att_send, att_recv, edge_sem, flip_sem, last_sem, core_sem, half_sem, zs_send, zs_recv, zq_send, zq_recv,
     zg_send, zg_recv, core2_sem,
@@ -642,20 +642,28 @@
     hbuf[...] = nbuf[0] + nbuf[1] + nbuf[2] + nbuf[3]
     half_copy = remote(hbuf, hbuf_in, half_sem.at[0], half_sem.at[1], f, p.mate)
     half_copy.start()
+    flip_copy.start()
+
+    @pl.when(own_last)
+    def _():
+        last_in[...] = last_out[...]
+
+    @pl.when(jnp.logical_not(own_last))
+    def _():
+        last_copy.start()
+
     half_copy.wait_recv()
     qbuf[q] = hbuf[...] + hbuf_in[...]
     for r in range(1, quads):
         i, there = far(r)
         remote(qbuf.at[q], qbuf.at[q], zq_send.at[r], zq_recv.at[q], f, there).start()
-    flip_copy.start()
-
-    @pl.when(own_last)
-    def _():
-        last_in[...] = last_out[...]
-
-    @pl.when(jnp.logical_not(own_last))
-    def _():
-        last_copy.start()
+    drain()
+
+    @pl.loop(1, F)
+    def _(r):
+        att_copy(r).wait_send()
+        remote(pp.at[0], rs.at[0], rs_send.at[r], rs_recv.at[0], lax.rem(f + r, F), c).wait_send()
+        remote(psum, pall.at[0], ag_send.at[r], ag_recv.at[0], lax.rem(f + r, F), c).wait_send()
 
     for r in range(1, quads):
         i, there = far(r)
@@ -680,12 +688,6 @@
     to_core.start()
     remote(full.at[1 - k], full.at[1 - k], core2_sem.at[0], core2_sem.at[1], f, p.sib).wait_recv()
     hg_ref[...] = full[...].reshape(hg_ref.shape)
-
-    @pl.loop(1, F)
-    def _(r):
-        att_copy(r).wait_send()
-        remote(pp.at[0], rs.at[0], rs_send.at[r], rs_recv.at[0], lax.rem(f + r, F), c).wait_send()
-        remote(psum, pall.at[0], ag_send.at[r], ag_recv.at[0], lax.rem(f + r, F), c).wait_send()
 
     for r in range(1, 4):
         i, there = near(r)
@@ -723,10 +725,8 @@
         copy.wait()
     early, drain = attend_phase(p, weights, *map(g, ATTEND))
     head_phase(
-        p, early, g("att"), g("wt"), g("stream"), g("sp"), g("m3"), g("lat"), flip_ref, hg_ref, *map(g, HEAD)
+        p, early, lambda: (drain(), weights.drain()), g("att"), g("wt"), g("stream"), g("sp"), g("m3"), g("lat"), flip_ref, hg_ref, *map(g, HEAD)
     )
-    drain()
-    weights.drain()
 
 
 WEIGHTS = (

time: 105 us -> 102 us (0.971)
  Pallas kernels: 101 us -> 98.1 us
    pallas_call x1, Pallas kernels: 101 us -> 98.1 us  [shards(): pl.pallas_call(functools.partial(kernel, F, C), out_shape=(jax.ShapeDtype...]
where the time goes in v6:
time: 102 us
  Pallas kernels  98.1 us (96%)
  local copies, waits for them, and re-layouts  2.99 us (3%)
    pallas_call x1, Pallas kernels, shards(): pl.pallas_call(functools.partial(kernel, F, C), out_shape=(jax.ShapeDtype...  98.1 us
    unnamed x2, local copies, waits for them, and re-layouts  2.99 us

profile of v6, /device:TPU:1, one launch (start us, length us, event | category | flops | bytes accessed | tf_op | source)
XLA Modules:
  0.0 101.7 jit_solution(563899425331259373)
XLA Ops:
  0.6 98.1 %coupling.1 = (f32[64,128]{1,0:T(8,128)}, f32[384,128]{1,0:T(8,128)}) custom-call(f32[64,128]{1,0:T(8,128)} %bitcast.5, bf16[128,3072]{1,0:T(8,128)(2,1)} %stream_hbm.1, bf16[128,256]{1,0:T(8,128)(2,1)} %q_hbm.1, bf16[128,256]{1,0:T(8,128)(2,1)} %k_hbm.1, bf16[128,256]{1,0:T(8,128)(2,1)} %v_hbm.1, bf16[48,256]{1,0:T(8,128)(2,1)} %bitcast.7, ...), custom_call_target="tpu_custom_call" | custom-call | tf_op jit(solution)/shard_map/coupling/pallas_call | solution.py:790
  98.7 1.4 %copy.11 = f32[128,64]{0,1:T(8,128)} copy(f32[128,64]{0,1:T(8,128)} %bitcast.6) | data formatting | bytes 65536
  100.1 1.6 %copy.12 = f32[384,128]{1,0:T(8,128)} copy(f32[384,128]{1,0:T(8,128)} %get-tuple-element.9) | data formatting | bytes 393216
